TPU v7x, 32 devices: a whole 2x2x4 slice. The times are simulated.
32 devices in a mesh: task: 16 (over z, x, core), tensor: 2 (over y).
Axes of the slice: x: 2, y: 2, z: 4, core: 2. Of those that a mesh axis runs over, the one named last changes fastest.
Arguments:
- inputs: bfloat16 [3072, 8192], P('task'), may hold values from -6 to 6
- queries: bfloat16 [3072, 4096], P('task', 'tensor'), may hold values from -6 to 6
- task_vectors: bfloat16 [8, 2, 8192, 1024], P(None, None, 'task', 'tensor'), may hold values from -0.0625 to 0.0625
- base_weights: bfloat16 [2, 8192, 1024], P(None, 'task', 'tensor'), may hold values from -0.0625 to 0.0625
- scale_exps: int32 [8, 2, 64, 8], P(None, None, 'task', 'tensor'), may hold values from -3 to 0
- coefs: float32 [8, 2], replicated, may hold values from 0.1 to 0.6
Outputs:
- attended: bfloat16 [3072, 4096], P('task', 'tensor')
- mean_entropy: float32 [], replicated
- coef_grad: float32 [8, 2], replicated
All inputs are finite; a program needn't handle non-finite values.
Results may differ from a plain program's by a relative error of at most 0.0087.
Values may be sent and summed in bfloat16 or wider, within the bound.
A program may use at most 128 MiB of HBM per device.

v0:
```python
import jax
import jax.numpy as jnp
from jax import lax
from jax.sharding import PartitionSpec as P

HEAD = 128
GROUP = 4


sharpen = 4.0
capping = 8.0
masked_value = -1e30


def dequantize(vectors, exponents):
    tasks, mats, rows, cols = vectors.shape
    row_blocks = exponents.shape[2]
    col_blocks = exponents.shape[3]
    factor = jnp.exp2(exponents.astype(jnp.float32))
    blocked = vectors.astype(jnp.float32).reshape(
        tasks, mats, row_blocks, rows // row_blocks, col_blocks, cols // col_blocks
    )
    blocked = blocked * factor[:, :, :, None, :, None]
    return blocked.reshape(tasks, mats, rows, cols)


def capped_logits(attended):
    return capping * jnp.tanh(sharpen * attended.astype(jnp.float32) / capping)


def entropy_grad(logits, expo, total, moment):
    average = moment / total
    entropy = jnp.log(total) - average
    slope = sharpen * (1.0 - (logits / capping) ** 2)
    d_out = (slope * (-(expo / total[:, None]) * (logits - average[:, None]))).astype(jnp.bfloat16)
    return (entropy, d_out)


def local(inputs, queries, task_vectors, base_weights, scale_exps, coefs):
    n_task = lax.axis_size("task")
    n_tensor = lax.axis_size("tensor")
    tok_count = inputs.shape[0]
    col_dev = task_vectors.shape[3]
    kv_local = col_dev // HEAD
    scaled = dequantize(task_vectors, scale_exps)
    merged = (
        base_weights.astype(jnp.float32) + jnp.sum(coefs[:, :, None, None] * scaled, axis=0)
    ).astype(jnp.bfloat16)
    projected = jnp.einsum(
        "td,mdc->mtc",
        inputs,
        lax.all_gather(merged, "task", axis=1, tiled=True),
        preferred_element_type=jnp.float32,
    )
    projected_b = projected.astype(jnp.bfloat16)
    keys_b = projected_b[0].reshape(tok_count, kv_local, HEAD)
    values_b = projected_b[1].reshape(tok_count, kv_local, HEAD)
    query_heads = queries.reshape(tok_count, kv_local, GROUP, HEAD)
    inverse = HEAD ** (-0.5)
    scores = (
        jnp.einsum("shrd,thd->hrst", query_heads, keys_b, preferred_element_type=jnp.float32)
        * inverse
    )
    position = jnp.arange(tok_count)
    causal = position[None, :] <= position[:, None]
    scores = jnp.where(causal, scores, masked_value)
    probs = jax.nn.softmax(scores, axis=-1)
    probs_b = probs.astype(jnp.bfloat16)
    outputs = jnp.einsum("hrst,thd->shrd", probs_b, values_b, preferred_element_type=jnp.float32)
    attended = outputs.astype(jnp.bfloat16).reshape(tok_count, kv_local * GROUP * HEAD)
    logits = capped_logits(attended)
    expo = jnp.exp(logits)
    total, moment = lax.psum((jnp.sum(expo, axis=1), jnp.sum(expo * logits, axis=1)), "tensor")
    entropy, d_out = entropy_grad(logits, expo, total, moment)
    entropy_part = jnp.sum(entropy) / n_tensor
    d_out_heads = d_out.reshape(tok_count, kv_local, GROUP, HEAD)
    d_probs = jnp.einsum(
        "shrd,thd->hrst", d_out_heads, values_b, preferred_element_type=jnp.float32
    )
    d_scores = (probs * (d_probs - jnp.sum(probs * d_probs, axis=-1, keepdims=True))).astype(
        jnp.bfloat16
    )
    d_keys = (
        jnp.einsum("hrst,shrd->thd", d_scores, query_heads, preferred_element_type=jnp.float32)
        * inverse
    )
    d_values = jnp.einsum(
        "hrst,shrd->thd", probs_b, d_out_heads, preferred_element_type=jnp.float32
    )
    d_kv = jnp.stack(
        [d_keys.reshape(tok_count, col_dev), d_values.reshape(tok_count, col_dev)]
    ).astype(jnp.bfloat16)
    input_rows = lax.all_to_all(inputs, "task", split_axis=1, concat_axis=0, tiled=True)
    weight_grads = jnp.einsum(
        "tr,mtc->mrc",
        input_rows,
        lax.all_gather(d_kv, "task", axis=1, tiled=True),
        preferred_element_type=jnp.float32,
    )
    coef_part = jnp.sum(weight_grads[None] * scaled, axis=(2, 3))
    entropy_sum, coef_grad = lax.psum((entropy_part, coef_part), ("task", "tensor"))
    mean_entropy = entropy_sum / (tok_count * n_task)
    return (attended, mean_entropy, coef_grad)


def solution(mesh):
    return jax.shard_map(
        local,
        mesh=mesh,
        in_specs=(
            P("task", None),
            P("task", "tensor"),
            P(None, None, "task", "tensor"),
            P(None, "task", "tensor"),
            P(None, None, "task", "tensor"),
            P(),
        ),
        out_specs=(P("task", "tensor"), P(), P()),
        check_vma=False,
    )
```

profile of v0, /device:TPU:0, one launch (start us, length us, event | category | flops | bytes accessed | tf_op | source)
XLA Modules:
  0.0 388.9 jit_solution(6853657786691911180)
XLA Ops:
  7.2 0.7 multiply_exponential_fusion
  8.1 6.1 %mul.78 = f32[8,2,4,128,4,128]{5,4,3,2,1,0:T(4,128)} broadcast(f32[8,2,4,4]{3,2,1,0:T(4,128)S(1)} %copy.33), dimensions={0,1,2,4} | broadcast | bytes 16778240 | tf_op jit(solution)/shard_map/mul | solution.py:23
  14.2 19.9 %mul.79 = f32[8,2,512,512]{3,2,1,0:T(8,128)} reshape(f32[8,2,4,128,4,128]{5,4,3,2,1,0:T(4,128)} %mul.78) | data formatting | bytes 33554432 | tf_op jit(solution)/shard_map/mul | solution.py:23
  34.2 9.7 %multiply_reduce_fusion.1 = f32[2,512,512]{2,1,0:T(8,128)S(1)} fusion(f32[8,2,512,512]{3,2,1,0:T(8,128)} %mul.79, bf16[8,2,512,512]{3,2,1,0:T(8,128)(2,1)} %param.8, f32[8,2]{1,0:T(8,128)S(1)} %copy.32), kind=kLoop, calls=%fused_computation.2 | loop fusion | flops 16252928 | bytes 27263040 | tf_op jit(solution)/shard_map/reduce_sum | solution.py:47
  43.9 1.4 add_convert_fusion
  45.3 3.0 reshape.37
  48.9 125.7 %all-gather.3.cloned.1.call-done = bf16[2,8192,512]{2,1,0:T(8,128)(2,1)} async-done(((bf16[2,512,512]{2,1,0:T(8,128)(2,1)}), bf16[2,8192,512]{2,1,0:T(8,128)(2,1)}) %all-gather.3.cloned.1.call-update) | async-done | bytes 16777232 | tf_op jit(solution)/shard_map/all_gather | solution.py:52
  174.6 7.6 %fusion.26 = bf16[2,192,512]{2,1,0:T(8,128)(2,1)S(1)} fusion(bf16[2,8192,512]{2,1,0:T(8,128)(2,1)} %all-gather.3.cloned.1.call-done, bf16[192,8192]{1,0:T(8,128)(2,1)S(1)} %copy-done), kind=kOutput, calls=%fused_computation.38 | convolution fusion | flops 3221422080 | bytes 20316160 | tf_op jit(solution)/shard_map/td,mdc->mtc/dot_general | solution.py:49
  182.2 0.7 fusion.53
  182.9 1.0 reshape_squeeze.7
  183.9 0.7 reshape_squeeze.6
  184.6 1.7 fusion.43
  186.4 1.0 fusion.54
  187.4 1.9 exponential_reduce_fusion
  189.4 4.9 %all-reduce.1 = (f32[192]{0:T(256)S(1)}, f32[192]{0:T(256)S(1)}) all-reduce(f32[192]{0:T(256)S(1)} %get-tuple-element.7, f32[192]{0:T(256)S(1)} %get-tuple-element.6), channel_id=1, replica_groups=mesh['task'=16,'tensor'=2] {'tensor'}, use_global_device_ids=true, to_apply=%region_6.7 | all-reduce | flops 384 | bytes 3072 | tf_op jit(solution)/shard_map/psum | solution.py:73
  194.9 3.6 fusion.1
  198.5 1.9 fusion.36
  200.5 0.9 fusion.37
  201.6 1.1 copy.42
  202.7 0.8 stack_reshape.9
  203.4 1.7 pad_maximum_fusion
  205.1 2.0 copy.74
  207.2 3.9 %all-to-all-start = ((bf16[192,16,512]{2,0,1:T(8,128)(2,1)}), bf16[192,16,512]{2,0,1:T(8,128)(2,1)S(1)}, u32[]{:S(2)}, u32[]{:S(2)}) async-start(bf16[192,16,512]{2,0,1:T(8,128)(2,1)} %bitcast.76), calls=%async_computation | async-start | bytes 6291456 | tf_op jit(solution)/shard_map/all_to_all | solution.py:93
  211.1 2.6 copy.38
  214.4 92.6 %all-to-all-done = bf16[192,16,512]{2,0,1:T(8,128)(2,1)S(1)} async-done(((bf16[192,16,512]{2,0,1:T(8,128)(2,1)}), bf16[192,16,512]{2,0,1:T(8,128)(2,1)S(1)}, u32[]{:S(2)}, u32[]{:S(2)}) %all-to-all-start) | async-done | bytes 3145760 | tf_op jit(solution)/shard_map/all_to_all | solution.py:93
  307.0 4.0 %all-gather.5.cloned.1.call-done = bf16[2,3072,512]{2,1,0:T(8,128)(2,1)} async-done(((bf16[2,192,512]{2,1,0:T(8,128)(2,1)}), bf16[2,3072,512]{2,1,0:T(8,128)(2,1)}) %all-gather.5.cloned.1.call-update) | async-done | bytes 6291472 | tf_op jit(solution)/shard_map/all_gather | solution.py:97
  311.0 7.6 %convolution_bitcast_fusion = f32[2,512,512]{1,2,0:T(8,128)} fusion(bf16[2,3072,512]{2,1,0:T(8,128)(2,1)} %all-gather.5.cloned.1.call-done, bf16[3072,512,1]{1,0,2:T(8,128)(2,1)S(1)} %bitcast.78), kind=kOutput, calls=%fused_computation.19 | convolution fusion | flops 3221225472 | bytes 11534336 | tf_op jit(solution)/shard_map/tr,mtc->mrc/dot_general | solution.py:94
  318.5 1.9 copy.44
  320.5 9.3 %multiply_reduce_fusion = f32[8,2]{1,0:T(8,128)S(1)} fusion(f32[8,2,512,512]{3,2,1,0:T(8,128)} %mul.79, bf16[8,2,512,512]{3,2,1,0:T(8,128)(2,1)} %param.8, f32[2,512,512]{2,1,0:T(8,128)S(1)} %copy.44), kind=kLoop, calls=%fused_computation.1 | loop fusion | flops 16777200 | bytes 27263040 | tf_op jit(solution)/shard_map/reduce_sum | solution.py:100
  329.8 1.5 reshape.38
  331.3 48.3 %all-reduce = (f32[]{:T(128)}, f32[8,2]{1,0:T(8,128)S(1)}) all-reduce(f32[]{:T(128)S(6)} %div.37, f32[8,2]{1,0:T(8,128)S(1)} %multiply_reduce_fusion), channel_id=1, replica_groups=mesh['task'=16,'tensor'=2] {'task','tensor'}, use_global_device_ids=true, to_apply=%region_8.9 | all-reduce | flops 17 | bytes 136 | tf_op jit(solution)/shard_map/psum | solution.py:101
  379.6 0.6 copy.45
  (30 shorter events, 1.8 us)
Async XLA Ops:
  7.2 167.4 %all-gather.3.cloned.1.call-start = ((), (), s32[]{:S(2)}) async-start(), calls=%async_computation.1 | async-start | bytes 17825792 | tf_op jit(solution)/shard_map/all_gather | solution.py:52
  14.2 19.9 %copy-start.7 = (f32[8,2]{0,1:T(2,128)S(1)}, f32[8,2]{0,1:T(2,128)}, u32[]{:S(2)}) copy-start(f32[8,2]{0,1:T(2,128)} %param.11) | copy-start | bytes 196
  34.2 9.7 %copy-start.3 = (bf16[2,512,512]{2,1,0:T(8,128)(2,1)S(1)}, bf16[2,512,512]{2,1,0:T(8,128)(2,1)}, u32[]{:S(2)}) copy-start(bf16[2,512,512]{2,1,0:T(8,128)(2,1)} %param.9) | copy-start | bytes 3145732
  43.9 130.7 %copy-start = (bf16[192,8192]{1,0:T(8,128)(2,1)S(1)}, bf16[192,8192]{1,0:T(8,128)(2,1)}, u32[]{:S(2)}) copy-start(bf16[192,8192]{1,0:T(8,128)(2,1)} %param.6) | copy-start | bytes 9437188
  45.3 265.7 %all-gather.5.cloned.1.call-start = ((), (), s32[]{:S(2)}) async-start(), calls=%async_computation.2 | async-start | bytes 6684672 | tf_op jit(solution)/shard_map/all_gather | solution.py:97
  184.6 1.8 copy-start.6
  186.4 1.1 copy-start.5
  187.4 1.9 copy-start.8
  194.9 3.6 copy-start.4
  194.9 3.6 copy-start.9
  198.5 1.9 copy-start.2
  207.2 99.8 %all-to-all-start = ((bf16[192,16,512]{2,0,1:T(8,128)(2,1)}), bf16[192,16,512]{2,0,1:T(8,128)(2,1)S(1)}, u32[]{:S(2)}, u32[]{:S(2)}) async-start(bf16[192,16,512]{2,0,1:T(8,128)(2,1)} %bitcast.76), calls=%async_computation | async-start | bytes 6291456 | tf_op jit(solution)/shard_map/all_to_all | solution.py:93
  320.5 9.3 %copy-start.1 = (bf16[192,4,4,128]{3,2,1,0:T(4,128)(2,1)S(1)}, bf16[192,4,4,128]{3,2,1,0:T(4,128)(2,1)}, u32[]{:S(2)}) copy-start(bf16[192,4,4,128]{3,2,1,0:T(4,128)(2,1)} %copy.38) | copy-start | bytes 2359300
Sparse Core Ops, SparseCore 0:
  45.4 129.1 all-gather.2
  205.3 105.6 all-gather.4
where the time goes:
time: 390 us; the launch traced here: 389 us
  waiting for transfers between devices  222 us (57%)
  blocking collectives  53.2 us (14%)
  local copies, waits for them, and re-layouts  42.4 us (11%)
  matrix products  25.2 us (6%)
  other arithmetic  25.1 us (6%)
  between operations  16.6 us (4%)
  starting transfers between devices  4 us (1%)
    all_gather x1, waiting for transfers between devices, local(): lax.all_gather(merged, 'task', axis=1, tiled=True)  126 us
    all_to_all x1, waiting for transfers between devices, local(): lax.all_to_all(inputs, 'task', split_axis=1, concat_axis=0, tiled=True)  92.6 us
    psum x1, blocking collectives, local(): lax.psum((entropy_part, coef_part), ('task', 'tensor'))  48.3 us
    mul x2, local copies, waits for them, and re-layouts, dequantize(): blocked = blocked * factor[:, :, :, None, :, None]  26 us
    reduce_sum x1, other arithmetic, local(): jnp.sum(coefs[:, :, None, None] * scaled, axis=0)  9.68 us
    reduce_sum x1, other arithmetic, local(): coef_part = jnp.sum(weight_grads[None] * scaled, axis=(2, 3))  9.33 us
  transfers between devices with their start and end apart: 3, of which 3 were waited for; matrix products, arithmetic and copies ran while one was open for 2% of the time, Pallas kernels for 0%

commit v1 on v0

v1 whole, which is shorter than its diff:
```python
import functools
import math

import jax
import jax.numpy as jnp
from jax import lax
from jax.experimental import pallas as pl
from jax.experimental.pallas import tpu as pltpu
from jax.sharding import PartitionSpec as P

HEAD = 128
GROUP = 4

sharpen = 4.0
capping = 8.0
masked_value = -1e30

MESH = pl.DeviceIdType.MESH
VMEM_BYTES = 60 * 1024 * 1024
F32 = jnp.float32
BF16 = jnp.bfloat16


def factors(n_task):
    outer = math.gcd(n_task, 4)
    mid = math.gcd(n_task // outer, 2)
    return outer, mid, n_task // (outer * mid)


def place(dims):
    _, mid, inner = dims
    task = lax.axis_index("task")
    rest = lax.rem(task, mid * inner)
    return task, task // (mid * inner), rest // inner, lax.rem(rest, inner)


def turned(value, step, size):
    return lax.rem(value + (step + size), size)


def index_of(dims, a, b, c):
    _, mid, inner = dims
    return (a * mid + b) * inner + c


def meet(peers):
    sem = pltpu.get_barrier_semaphore()
    for peer in peers:
        pl.semaphore_signal(sem, inc=1, device_id=peer, device_id_type=MESH)
    pl.semaphore_wait(sem, len(peers))


def send(src, dst, send_sem, recv_sem, peer):
    copy = pltpu.make_async_remote_copy(
        src_ref=src,
        dst_ref=dst,
        send_sem=send_sem,
        recv_sem=recv_sem,
        device_id=peer,
        device_id_type=MESH,
    )
    copy.start()
    return copy


def fetch(src, dst, sem):
    copy = pltpu.make_async_copy(src, dst, sem)
    copy.start()
    return copy


def project_kernel(
    dims, n_tensor, row_blocks, col_blocks,
    inputs, vectors, base, scales,
    kv_out, rows_out,
    xin, mg, vec_v, base_v, acc, pout, pin,
    local_sem, keep_sem, x_send, x_recv, y_send, y_recv, g_send, g_recv, r_send, r_recv, p_send, p_recv,
):
    outer, mid, inner = dims
    group = mid * inner
    task, a, b, c = place(dims)
    y = lax.axis_index("tensor")
    mine = b * inner + c
    tasks, mats, rows, cols = vectors.shape
    span = group * rows
    part = span // n_tensor

    def at(a_, b_, c_):
        return {"task": index_of(dims, a_, b_, c_), "tensor": y}

    def tensor_peer(step):
        return {"task": task, "tensor": turned(y, step, n_tensor)}

    def group_peer(f, e):
        return at(a, turned(b, f, mid), turned(c, e, inner))

    peers = [at(turned(a, d, outer), b, c) for d in range(1, outer)]
    peers += [group_peer(f, e) for f in range(mid) for e in range(inner) if f or e]
    peers += [tensor_peer(s) for s in range(1, n_tensor)]
    vec_copy = fetch(vectors, vec_v, local_sem.at[0])
    base_copy = fetch(base, base_v, local_sem.at[1])
    own_copy = fetch(
        inputs.at[:, pl.ds(pl.multiple_of(a * span, 128), span)], xin.at[a], local_sem.at[2]
    )
    meet(peers)
    sent = []
    x_copies = {}
    own_cols = pl.ds(pl.multiple_of(y * part, 128), part)
    for d in range(1, outer):
        to = turned(a, d, outer)
        x_copies[d] = send(
            inputs.at[:, pl.ds(pl.multiple_of(to * span + y * part, 128), part)],
            xin.at[a, :, own_cols],
            x_send.at[d], x_recv.at[d], at(to, b, c),
        )
        sent.append(x_copies[d])
    base_copy.wait()
    vec_copy.wait()
    high = rows // row_blocks
    wide = cols // col_blocks

    def merge(step, carry):
        m = step // row_blocks
        i = lax.rem(step, row_blocks)
        these = pl.ds(pl.multiple_of(i * high, 8), high)
        for j in range(col_blocks):
            across = slice(j * wide, (j + 1) * wide)
            total = base_v[m, these, across].astype(F32)
            for t in range(tasks):
                scale = scales[((t * mats + m) * row_blocks + i) * col_blocks + j]
                total += scale * vec_v[t, m, these, across].astype(F32)
            mg[mine, m, these, across] = total.astype(BF16)
        return carry

    lax.fori_loop(0, mats * row_blocks, merge, 0)

    g_copies = {}
    for f in range(1, mid):
        g_copies[f, 0] = send(
            mg.at[mine], mg.at[mine], g_send.at[f * inner], g_recv.at[f * inner], group_peer(f, 0)
        )
    for e in range(1, inner):
        g_copies[0, e] = send(mg.at[mine], mg.at[mine], g_send.at[e], g_recv.at[e], group_peer(0, e))
    y_copies = {}

    def pass_on(d):
        x_copies[d].wait_recv()
        block = xin.at[turned(a, -d, outer), :, own_cols]
        for s in range(1, n_tensor):
            slot = d * n_tensor + s
            y_copies[d, s] = send(block, block, y_send.at[slot], y_recv.at[slot], tensor_peer(s))
            sent.append(y_copies[d, s])

    for f in range(1, mid):
        g_copies[f, 0].wait_recv()
        came = turned(b, -f, mid) * inner + c
        for e in range(1, inner):
            slot = f * inner + e
            g_copies[f, e] = send(
                mg.at[came], mg.at[came], g_send.at[slot], g_recv.at[slot], group_peer(0, e)
            )
    sent.extend(g_copies.values())

    def spread(d):
        a_from = turned(a, -d, outer)
        owner = a_from * group + mine
        for f in range(mid):
            for e in range(inner):
                if not (f or e):
                    continue
                to = turned(b, f, mid) * inner + turned(c, e, inner)
                slot = (d * mid + f) * inner + e
                r_copies.append(
                    send(
                        xin.at[a_from, :, pl.ds(pl.multiple_of(to * rows, 128), rows)],
                        rows_out.at[owner],
                        r_send.at[slot], r_recv.at[slot], group_peer(f, e),
                    )
                )
        keeps.append(
            fetch(
                xin.at[a_from, :, pl.ds(pl.multiple_of(mine * rows, 128), rows)],
                rows_out.at[owner],
                keep_sem.at[d],
            )
        )

    def product(d, m):
        a_from = turned(a, -d, outer)
        total = None
        for k in range(group):
            term = jnp.dot(
                xin[a_from, :, k * rows:(k + 1) * rows], mg[k, m], preferred_element_type=F32
            )
            total = term if total is None else total + term
        return total

    r_copies = []
    keeps = []
    own_copy.wait()
    spread(0)
    for f in range(mid):
        for e in range(1, inner):
            g_copies[f, e].wait_recv()
    for m in range(mats):
        acc[m] = product(0, m)
    p_copies = []
    if outer > 1:
        pass_on(1)
    for d in range(1, outer):
        if d + 1 < outer:
            pass_on(d + 1)
        for s in range(1, n_tensor):
            y_copies[d, s].wait_recv()
        for m in range(mats):
            pout[d, m] = product(d, m).astype(BF16)
        p_copies.append(
            send(pout.at[d], pin.at[d], p_send.at[d], p_recv.at[d], at(turned(a, -d, outer), b, c))
        )
        spread(d)
    for d, copy in enumerate(p_copies, 1):
        copy.wait_recv()
        for m in range(mats):
            acc[m] += pin[d, m].astype(F32)
    for m in range(mats):
        kv_out[m] = acc[m].astype(BF16)
    for copy in keeps:
        copy.wait()
    for copy in r_copies:
        copy.wait_recv()
    for copy in sent + p_copies + r_copies:
        copy.wait_send()


def project(dims, n_tensor, inputs, vectors, base, scales, blocks):
    outer, mid, inner = dims
    group = mid * inner
    tokens = inputs.shape[0]
    _, mats, rows, cols = vectors.shape
    span = group * rows
    dma = pltpu.SemaphoreType.DMA
    count = outer * group
    return pl.pallas_call(
        functools.partial(project_kernel, dims, n_tensor, *blocks),
        out_shape=(
            jax.ShapeDtypeStruct((mats, tokens, cols), BF16),
            jax.ShapeDtypeStruct((count, tokens, rows), BF16),
        ),
        in_specs=[
            pl.BlockSpec(memory_space=pl.ANY),
            pl.BlockSpec(memory_space=pl.ANY),
            pl.BlockSpec(memory_space=pl.ANY),
            pl.BlockSpec(memory_space=pltpu.SMEM),
        ],
        out_specs=(pl.BlockSpec(memory_space=pltpu.VMEM), pl.BlockSpec(memory_space=pl.ANY)),
        scratch_shapes=[
            pltpu.VMEM((outer, tokens, span), BF16),
            pltpu.VMEM((group, mats, rows, cols), BF16),
            pltpu.VMEM(vectors.shape, BF16),
            pltpu.VMEM(base.shape, BF16),
            pltpu.VMEM((mats, tokens, cols), F32),
            pltpu.VMEM((outer, mats, tokens, cols), BF16),
            pltpu.VMEM((outer, mats, tokens, cols), BF16),
            dma((3,)), dma((outer,)),
            dma((outer,)), dma((outer,)),
            dma((outer * n_tensor,)), dma((outer * n_tensor,)),
            dma((group,)), dma((group,)),
            dma((count,)), dma((count,)),
            dma((outer,)), dma((outer,)),
        ],
        compiler_params=pltpu.CompilerParams(
            collective_id=0, has_side_effects=True, vmem_limit_bytes=VMEM_BYTES
        ),
        name="project",
    )(inputs, vectors, base, scales)


def attend_kernel(
    n_tensor, queries, kv, att_out, dkv_out, ent_out, probs, logs, expos, sums, s_send, s_recv
):
    task = lax.axis_index("task")
    y = lax.axis_index("tensor")
    tokens = queries.shape[0]
    heads = kv.shape[2] // HEAD
    inverse = HEAD ** (-0.5)
    peers = [{"task": task, "tensor": turned(y, s, n_tensor)} for s in range(1, n_tensor)]
    if peers:
        meet(peers)
    key_at = lax.broadcasted_iota(jnp.int32, (tokens, GROUP * tokens), 0)
    query_at = lax.rem(lax.broadcasted_iota(jnp.int32, (tokens, GROUP * tokens), 1), tokens)
    causal = key_at <= query_at

    def stacked(h):
        return jnp.concatenate(
            [queries[:, (h * GROUP + r) * HEAD:(h * GROUP + r + 1) * HEAD] for r in range(GROUP)],
            axis=0,
        )

    total = jnp.zeros((tokens, HEAD), F32)
    moment = jnp.zeros((tokens, HEAD), F32)
    for h in range(heads):
        cut = slice(h * HEAD, (h + 1) * HEAD)
        scores = lax.dot_general(
            kv[0, :, cut], stacked(h), (((1,), (1,)), ((), ())), preferred_element_type=F32
        ) * inverse
        scores = jnp.where(causal, scores, masked_value)
        weight = jnp.exp(scores - jnp.max(scores, axis=0, keepdims=True))
        prob = weight * (1.0 / jnp.sum(weight, axis=0, keepdims=True))
        probs[h] = prob
        att = lax.dot_general(
            prob.astype(BF16), kv[1, :, cut], (((0,), (0,)), ((), ())), preferred_element_type=F32
        ).astype(BF16)
        logits = capping * jnp.tanh(sharpen * att.astype(F32) / capping)
        expo = jnp.exp(logits)
        logs[h] = logits
        expos[h] = expo
        scaled = expo * logits
        for r in range(GROUP):
            here = slice(r * tokens, (r + 1) * tokens)
            att_out[:, (h * GROUP + r) * HEAD:(h * GROUP + r + 1) * HEAD] = att[here]
            total += expo[here]
            moment += scaled[here]
    sums[y] = jnp.concatenate(
        [
            jnp.sum(total.T, axis=0, keepdims=True),
            jnp.sum(moment.T, axis=0, keepdims=True),
            jnp.zeros((6, tokens), F32),
        ],
        axis=0,
    )
    copies = [
        send(sums.at[y], sums.at[y], s_send.at[s], s_recv.at[s], peer)
        for s, peer in enumerate(peers)
    ]
    for copy in copies:
        copy.wait_recv()
    whole = sums[0]
    for s in range(1, n_tensor):
        whole = whole + sums[s]
    over = 1.0 / whole[0:1]
    average = whole[1:2] * over
    ent_out[...] = jnp.log(whole[0:1]) - average
    over_col = jnp.broadcast_to(over, (HEAD, tokens)).T
    average_col = jnp.broadcast_to(average, (HEAD, tokens)).T
    over_all = jnp.concatenate([over_col] * GROUP, axis=0)
    average_all = jnp.concatenate([average_col] * GROUP, axis=0)
    for h in range(heads):
        cut = slice(h * HEAD, (h + 1) * HEAD)
        logits = logs[h]
        slope = sharpen * (1.0 - (logits / capping) ** 2)
        d_out = (slope * (-(expos[h] * over_all) * (logits - average_all))).astype(BF16)
        prob = probs[h]
        d_probs = lax.dot_general(
            kv[1, :, cut], d_out, (((1,), (1,)), ((), ())), preferred_element_type=F32
        )
        d_scores = (
            prob * (d_probs - jnp.sum(prob * d_probs, axis=0, keepdims=True))
        ).astype(BF16)
        d_keys = jnp.dot(d_scores, stacked(h), preferred_element_type=F32) * inverse
        d_values = jnp.dot(prob.astype(BF16), d_out, preferred_element_type=F32)
        dkv_out[0, :, cut] = d_keys.astype(BF16)
        dkv_out[1, :, cut] = d_values.astype(BF16)
    for copy in copies:
        copy.wait_send()


def attend(n_tensor, queries, kv):
    tokens = queries.shape[0]
    heads = kv.shape[2] // HEAD
    vmem = pl.BlockSpec(memory_space=pltpu.VMEM)
    dma = pltpu.SemaphoreType.DMA
    return pl.pallas_call(
        functools.partial(attend_kernel, n_tensor),
        out_shape=(
            jax.ShapeDtypeStruct(queries.shape, BF16),
            jax.ShapeDtypeStruct(kv.shape, BF16),
            jax.ShapeDtypeStruct((1, tokens), F32),
        ),
        in_specs=[vmem, vmem],
        out_specs=(vmem, vmem, vmem),
        scratch_shapes=[
            pltpu.VMEM((heads, tokens, GROUP * tokens), F32),
            pltpu.VMEM((heads, GROUP * tokens, HEAD), F32),
            pltpu.VMEM((heads, GROUP * tokens, HEAD), F32),
            pltpu.VMEM((n_tensor, 8, tokens), F32),
            dma((n_tensor,)), dma((n_tensor,)),
        ],
        compiler_params=pltpu.CompilerParams(
            collective_id=1, has_side_effects=True, vmem_limit_bytes=VMEM_BYTES
        ),
        name="attend",
    )(queries, kv)


def reduce_kernel(
    dims, n_tensor, row_blocks, col_blocks,
    dkv, rows_in, vectors, factor, ent, out,
    got, rows_v, vec_v, grads, held, held_t,
    local_sem, g_send, g_recv, t_send, t_recv, y_send, y_recv,
):
    outer, mid, inner = dims
    n_task = outer * mid * inner
    task, a, b, c = place(dims)
    y = lax.axis_index("tensor")
    tasks, mats, rows, cols = vectors.shape

    rows_copy = fetch(rows_in, rows_v, local_sem.at[0])
    vec_copy = fetch(vectors, vec_v, local_sem.at[1])

    def to(d, f, e):
        spot = index_of(dims, turned(a, d, outer), turned(b, f, mid), turned(c, e, inner))
        return {"task": spot, "tensor": y}

    def source(d, f, e):
        return index_of(dims, turned(a, -d, outer), turned(b, -f, mid), turned(c, -e, inner))

    task_peers = [{"task": turned(task, s, n_task), "tensor": y} for s in range(1, n_task)]
    tensor_peers = [{"task": task, "tensor": turned(y, s, n_tensor)} for s in range(1, n_tensor)]
    meet(task_peers + tensor_peers)
    copies = {}

    def forward(held_at, hop):
        d, f, e = held_at
        where = source(d, f, e)
        slot = tuple(p + q for p, q in zip(held_at, hop))
        flat = (slot[0] * mid + slot[1]) * inner + slot[2]
        copies[slot] = send(
            got.at[where] if any(held_at) else dkv,
            got.at[where],
            g_send.at[flat], g_recv.at[flat], to(*hop),
        )

    def take(slot):
        if any(slot):
            copies[slot].wait_recv()
            block = got.at[source(*slot)]
        else:
            block = dkv
        d, f, e = slot
        if not e:
            if not f:
                for step in range(1, mid):
                    forward(slot, (0, step, 0))
            for step in range(1, inner):
                forward(slot, (0, 0, step))
        return block

    def gather(block, where, first):
        left = rows_v[where]
        for m in range(mats):
            term = lax.dot_general(
                left, block[m], (((0,), (0,)), ((), ())), preferred_element_type=F32
            )
            if first:
                grads[m] = term
            else:
                grads[m] += term

    for d in range(1, outer):
        forward((0, 0, 0), (d, 0, 0))
    rows_copy.wait()
    for step in range(outer + 2):
        slots = []
        if step < outer:
            slots.append((step, 0, 0))
        if 1 <= step <= outer:
            slots += [(step - 1, f, 0) for f in range(1, mid)]
            slots += [(step - 1, 0, e) for e in range(1, inner)]
        if step >= 2:
            slots += [(step - 2, f, e) for f in range(1, mid) for e in range(1, inner)]
        for slot in slots:
            gather(take(slot), source(*slot), not any(slot))
    vec_copy.wait()
    high = rows // row_blocks
    wide = cols // col_blocks
    lines = []
    for m in range(mats):
        def contract(i, carry):
            these = pl.ds(pl.multiple_of(i * high, 8), high)
            carry = list(carry)
            for j in range(col_blocks):
                across = slice(j * wide, (j + 1) * wide)
                grad = grads[m, these, across]
                for t in range(tasks):
                    scale = factor[((t * mats + m) * row_blocks + i) * col_blocks + j]
                    term = grad * vec_v[t, m, these, across].astype(F32)
                    term = jnp.sum(term.reshape(high // 8, 8, wide), axis=0)
                    carry[t] = carry[t] + scale * term
            return tuple(carry)

        start = tuple(jnp.zeros((8, wide), F32) for _ in range(tasks))
        lines.append(lax.fori_loop(0, row_blocks, contract, start))
    parts = [
        jnp.sum(lines[m][t], axis=0, keepdims=True) for t in range(tasks) for m in range(mats)
    ]
    entropy = jnp.broadcast_to(jnp.sum(ent[...]) / (n_tensor * wide), (1, wide))
    pad = held.shape[1] - len(parts) - 1
    held[task] = jnp.concatenate(parts + [entropy, jnp.zeros((pad, wide), F32)], axis=0)
    last = [
        send(held.at[task], held.at[task], t_send.at[s], t_recv.at[s], peer)
        for s, peer in enumerate(task_peers)
    ]
    for copy in last:
        copy.wait_recv()
    total = held[0]
    for k in range(1, n_task):
        total = total + held[k]
    held_t[y] = total
    more = [
        send(held_t.at[y], held_t.at[y], y_send.at[s], y_recv.at[s], peer)
        for s, peer in enumerate(tensor_peers)
    ]
    for copy in more:
        copy.wait_recv()
    total = held_t[0]
    for k in range(1, n_tensor):
        total = total + held_t[k]
    out[...] = jnp.sum(total, axis=1, keepdims=True)
    for copy in list(copies.values()) + last + more:
        copy.wait_send()


def reduce(dims, n_tensor, dkv, rows_in, vectors, factor, ent, blocks):
    n_task, tokens, rows = rows_in.shape
    tasks, mats, _, cols = vectors.shape
    wide = cols // blocks[1]
    lines = -(-(tasks * mats + 1) // 8) * 8
    vmem = pl.BlockSpec(memory_space=pltpu.VMEM)
    hbm = pl.BlockSpec(memory_space=pl.ANY)
    dma = pltpu.SemaphoreType.DMA
    return pl.pallas_call(
        functools.partial(reduce_kernel, dims, n_tensor, *blocks),
        out_shape=jax.ShapeDtypeStruct((lines, 1), F32),
        in_specs=[vmem, hbm, hbm, pl.BlockSpec(memory_space=pltpu.SMEM), vmem],
        out_specs=vmem,
        scratch_shapes=[
            pltpu.VMEM((n_task, mats, tokens, cols), BF16),
            pltpu.VMEM((n_task, tokens, rows), BF16),
            pltpu.VMEM(vectors.shape, BF16),
            pltpu.VMEM((mats, rows, cols), F32),
            pltpu.VMEM((n_task, lines, wide), F32),
            pltpu.VMEM((n_tensor, lines, wide), F32),
            dma((2,)),
            dma((n_task,)), dma((n_task,)),
            dma((n_task,)), dma((n_task,)),
            dma((n_tensor,)), dma((n_tensor,)),
        ],
        compiler_params=pltpu.CompilerParams(
            collective_id=2, has_side_effects=True, vmem_limit_bytes=VMEM_BYTES
        ),
        name="reduce",
    )(dkv, rows_in, vectors, factor, ent)


def local(inputs, queries, task_vectors, base_weights, scale_exps, coefs):
    n_task = lax.axis_size("task")
    n_tensor = lax.axis_size("tensor")
    dims = factors(n_task)
    tasks, mats = coefs.shape
    blocks = scale_exps.shape[2:]
    factor = jnp.exp2(scale_exps.astype(F32))
    scales = coefs[:, :, None, None] * factor
    kv, rows_in = project(
        dims, n_tensor, inputs, task_vectors, base_weights, scales.reshape(-1), blocks
    )
    attended, dkv, ent = attend(n_tensor, queries, kv)
    sums = reduce(dims, n_tensor, dkv, rows_in, task_vectors, factor.reshape(-1), ent, blocks)
    coef_grad = sums[: tasks * mats, 0].reshape(tasks, mats)
    mean_entropy = sums[tasks * mats, 0] / (inputs.shape[0] * n_task)
    return (attended, mean_entropy, coef_grad)


def solution(mesh):
    return jax.shard_map(
        local,
        mesh=mesh,
        in_specs=(
            P("task", None),
            P("task", "tensor"),
            P(None, None, "task", "tensor"),
            P(None, "task", "tensor"),
            P(None, None, "task", "tensor"),
            P(),
        ),
        out_specs=(P("task", "tensor"), P(), P()),
        check_vma=False,
    )
```

time: 390 us -> 173 us (0.44)
  waiting for transfers between devices: 222 us -> 0 us
  Pallas kernels: 0 us -> 164 us
  blocking collectives: 53.2 us -> 0 us
  local copies, waits for them, and re-layouts: 42.4 us -> 5.22 us
  matrix products: 25.2 us -> 0 us
  other arithmetic: 25.1 us -> 0.73 us
  between operations: 16.6 us -> 2.45 us
  starting transfers between devices: 4 us -> 0 us
    pallas_call x0 -> x3, Pallas kernels: none -> 164 us  [the longest x1 85.5 us: project(): pl.pallas_call(functools.partial(project_kernel, dims, n_tensor, *blocks)...]
    all_gather x2 -> x0, waiting for transfers between devices: 130 us -> none  [the longest x1 126 us: local(): lax.all_gather(merged, 'task', axis=1, tiled=True)]
    all_to_all x1 -> x0, waiting for transfers between devices: 92.6 us -> none  [local(): lax.all_to_all(inputs, 'task', split_axis=1, concat_axis=0, tiled=True)]
    psum x2 -> x0, blocking collectives: 53.2 us -> none  [the longest x1 48.3 us: local(): lax.psum((entropy_part, coef_part), ('task', 'tensor'))]
    mul x3 -> x1, local copies, waits for them, and re-layouts: 26.2 us -> 0.13 us  [local(): scales = coefs[:, :, None, None] * factor]
    dot_general x7 -> x0, matrix products: 25.2 us -> none  [the longest x1 7.62 us: local(): jnp.einsum('td,mdc->mtc', inputs, lax.all_gather(merged, 'task', axis=1,...]
    reduce_sum x3 -> x0, other arithmetic: 19.6 us -> none  [the longest x1 9.68 us: local(): jnp.sum(coefs[:, :, None, None] * scaled, axis=0)]
    all_to_all x1 -> x0, starting transfers between devices: 3.92 us -> none  [local(): lax.all_to_all(inputs, 'task', split_axis=1, concat_axis=0, tiled=True)]
  transfers between devices with their start and end apart: 3 -> 0, of which waited for: 3 -> 0; matrix products, arithmetic and copies ran while one was open for 2% -> 0% of each run, Pallas kernels for 0% -> 0%
where the time goes in v1:
time: 173 us
  Pallas kernels  164 us (95%)
  local copies, waits for them, and re-layouts  5.22 us (3%)
  between operations  2.45 us (1%)
    pallas_call x1, Pallas kernels, project(): pl.pallas_call(functools.partial(project_kernel, dims, n_tensor, *blocks)...  85.5 us
    pallas_call x1, Pallas kernels, reduce(): pl.pallas_call(functools.partial(reduce_kernel, dims, n_tensor, *blocks),...  69.1 us
    pallas_call x1, Pallas kernels, attend(): pl.pallas_call(functools.partial(attend_kernel, n_tensor), out_shape=(jax...  9.74 us

profile of v1, /device:TPU:0, one launch (start us, length us, event | category | flops | bytes accessed | tf_op | source)
XLA Modules:
  0.0 172.7 jit_solution(7694350812448992779)
XLA Ops:
  0.6 0.7 multiply_exponential_fusion
  1.4 0.1 copy.11
  1.5 0.7 reshape.16.factor
  2.2 0.1 copy.10
  2.3 0.7 reshape.15.scales
  3.0 85.5 %project.1 = (bf16[2,192,512]{2,1,0:T(8,128)(2,1)}, bf16[16,192,512]{2,1,0:T(8,128)(2,1)}) custom-call(bf16[192,8192]{1,0:T(8,128)(2,1)} %inputs.1, bf16[8,2,512,512]{3,2,1,0:T(8,128)(2,1)} %vectors.3, bf16[2,512,512]{2,1,0:T(8,128)(2,1)} %base.1, f32[256]{0:T(256)} %reshape.15.scales), custom_call_target="tpu_custom_call" | custom-call | tf_op jit(solution)/shard_map/project/pallas_call | solution.py:243
  88.5 9.7 %attend.1 = (bf16[192,2048]{1,0:T(8,128)(2,1)}, bf16[2,192,512]{2,1,0:T(8,128)(2,1)}, f32[1,192]{1,0:T(1,128)}) custom-call(bf16[192,2048]{1,0:T(8,128)(2,1)} %queries.1, bf16[2,192,512]{2,1,0:T(8,128)(2,1)} %get-tuple-element.8.kv), custom_call_target="tpu_custom_call" | custom-call | tf_op jit(solution)/shard_map/attend/pallas_call | solution.py:372
  98.2 0.0 copy-start
  98.2 69.1 %reduce.3 = f32[24,1]{1,0:T(8,128)} custom-call(bf16[2,192,512]{2,1,0:T(8,128)(2,1)} %get-tuple-element.10.dkv, bf16[16,192,512]{2,1,0:T(8,128)(2,1)} %get-tuple-element.11.rows_in, bf16[8,2,512,512]{3,2,1,0:T(8,128)(2,1)} %vectors.3, f32[256]{0:T(256)} %reshape.16.factor, f32[1,192]{1,0:T(1,128)} %get-tuple-element.12.ent), custom_call_target="tpu_custom_call" | custom-call | tf_op jit(solution)/shard_map/reduce/pallas_call | solution.py:531
  167.3 1.2 slice.6
  169.2 0.8 slice_reduce_fusion
  170.0 0.1 reshape_squeeze.3
  170.1 0.6 copy.12
  170.7 0.0 copy-done
  170.7 0.9 copy.14
Async XLA Ops:
  98.2 72.5 %copy-start = (bf16[192,2048]{1,0:T(8,128)(2,1)S(1)}, bf16[192,2048]{1,0:T(8,128)(2,1)}, u32[]{:S(2)}) copy-start(bf16[192,2048]{1,0:T(8,128)(2,1)} %get-tuple-element.24) | copy-start | bytes 2359300

commit v2 on v1

v2 whole, which is shorter than its diff:
```python
import functools
import math

import jax
import jax.numpy as jnp
from jax import lax
from jax.experimental import pallas as pl
from jax.experimental.pallas import tpu as pltpu
from jax.sharding import PartitionSpec as P

HEAD = 128
GROUP = 4

sharpen = 4.0
capping = 8.0
masked_value = -1e30

MESH = pl.DeviceIdType.MESH
VMEM_BYTES = 60 * 1024 * 1024
F32 = jnp.float32
BF16 = jnp.bfloat16


def factors(n_task):
    outer = math.gcd(n_task, 4)
    mid = math.gcd(n_task // outer, 2)
    return outer, mid, n_task // (outer * mid)


def place(dims):
    _, mid, inner = dims
    task = lax.axis_index("task")
    rest = lax.rem(task, mid * inner)
    return task, task // (mid * inner), rest // inner, lax.rem(rest, inner)


def turned(value, step, size):
    return lax.rem(value + (step + size), size)


def flip(value, step):
    bit = 1
    for_value = value
    while bit <= step:
        if step & bit:
            for_value = for_value + bit - 2 * bit * lax.rem(value // bit, 2)
        bit *= 2
    return for_value


def scale_of(exps, t, m, i, j):
    return lax.shift_left(jnp.int32(1), exps[t, m, i, j] + 3).astype(F32) * 0.125


def index_of(dims, a, b, c):
    _, mid, inner = dims
    return (a * mid + b) * inner + c


def meet(peers):
    sem = pltpu.get_barrier_semaphore()
    for peer in peers:
        pl.semaphore_signal(sem, inc=1, device_id=peer, device_id_type=MESH)
    pl.semaphore_wait(sem, len(peers))


def send(src, dst, send_sem, recv_sem, peer):
    copy = pltpu.make_async_remote_copy(
        src_ref=src,
        dst_ref=dst,
        send_sem=send_sem,
        recv_sem=recv_sem,
        device_id=peer,
        device_id_type=MESH,
    )
    copy.start()
    return copy


def fetch(src, dst, sem):
    copy = pltpu.make_async_copy(src, dst, sem)
    copy.start()
    return copy


def project_kernel(
    dims, n_tensor, pieces,
    inputs, vectors, base, exps, coefs,
    kv_out, rows_out,
    xin, mg, vec_v, base_v, acc, hold, pout, pin,
    local_sem, keep_sem, x_send, x_recv, y_send, y_recv, g_send, g_recv, r_send, r_recv, p_send, p_recv,
):
    outer, mid, inner = dims
    group = mid * inner
    task, a, b, c = place(dims)
    y = lax.axis_index("tensor")
    mine = b * inner + c
    tasks, mats, rows, cols = vectors.shape
    row_blocks, col_blocks = exps.shape[2:]
    tokens = inputs.shape[0]
    piece = tokens // pieces
    span = group * rows
    part = span // n_tensor
    turns = list(range(outer - 1, 0, -1))

    def at(a_, b_, c_):
        return {"task": index_of(dims, a_, b_, c_), "tensor": y}

    def tensor_peer(step):
        return {"task": task, "tensor": turned(y, step, n_tensor)}

    def group_peer(f, e):
        return at(a, turned(b, f, mid), turned(c, e, inner))

    def some(k):
        return slice(k * piece, (k + 1) * piece)

    peers = [at(flip(a, d), b, c) for d in turns]
    peers += [group_peer(f, e) for f in range(mid) for e in range(inner) if f or e]
    peers += [tensor_peer(s) for s in range(1, n_tensor)]
    base_copy = fetch(base, base_v, local_sem.at[0])
    vec_copies = [
        fetch(vectors.at[:, m], vec_v.at[:, m], local_sem.at[2 + m]) for m in range(mats)
    ]
    own_copy = fetch(
        inputs.at[:, pl.ds(pl.multiple_of(a * span, 128), span)], xin.at[a], local_sem.at[1]
    )
    meet(peers)
    sent = []
    x_copies = {}
    own_cols = pl.ds(pl.multiple_of(y * part, 128), part)
    for k in range(pieces):
        for d in turns:
            to = flip(a, d)
            slot = d * pieces + k
            x_copies[k, d] = send(
                inputs.at[some(k), pl.ds(pl.multiple_of(to * span + y * part, 128), part)],
                xin.at[a, some(k), own_cols],
                x_send.at[slot], x_recv.at[slot], at(to, b, c),
            )
            sent.append(x_copies[k, d])
    high = rows // row_blocks
    wide = cols // col_blocks
    base_copy.wait()
    g_copies = {}

    def share(m, f, e, hop):
        came = turned(b, -(f - hop[0]), mid) * inner + turned(c, -(e - hop[1]), inner)
        slot = (m * mid + f) * inner + e
        g_copies[m, f, e] = send(
            mg.at[came, m], mg.at[came, m], g_send.at[slot], g_recv.at[slot], group_peer(*hop)
        )
        sent.append(g_copies[m, f, e])

    for m in range(mats):
        vec_copies[m].wait()

        def merge(i, carry):
            these = pl.ds(pl.multiple_of(i * high, 8), high)
            for j in range(col_blocks):
                across = slice(j * wide, (j + 1) * wide)
                total = base_v[m, these, across].astype(F32)
                for t in range(tasks):
                    scale = coefs[t, m] * scale_of(exps, t, m, i, j)
                    total += scale * vec_v[t, m, these, across].astype(F32)
                mg[mine, m, these, across] = total.astype(BF16)
            return carry

        lax.fori_loop(0, row_blocks, merge, 0)
        for f in range(1, mid):
            share(m, f, 0, (f, 0))
        for e in range(1, inner):
            share(m, 0, e, (0, e))

    r_copies = []
    keeps = []

    def spread(k, d):
        a_from = flip(a, d)
        owner = a_from * group + mine
        for f in range(mid):
            for e in range(inner):
                if not (f or e):
                    continue
                to = turned(b, f, mid) * inner + turned(c, e, inner)
                slot = ((k * outer + d) * mid + f) * inner + e
                r_copies.append(
                    send(
                        xin.at[a_from, some(k), pl.ds(pl.multiple_of(to * rows, 128), rows)],
                        rows_out.at[owner, some(k)],
                        r_send.at[slot], r_recv.at[slot], group_peer(f, e),
                    )
                )
        keeps.append(
            fetch(
                xin.at[a_from, some(k), pl.ds(pl.multiple_of(mine * rows, 128), rows)],
                rows_out.at[owner, some(k)],
                keep_sem.at[k * outer + d],
            )
        )

    y_copies = {}

    def pass_on(k):
        for d in turns:
            x_copies[k, d].wait_recv()
            block = xin.at[flip(a, d), some(k), own_cols]
            for s in range(1, n_tensor):
                slot = (k * outer + d) * n_tensor + s
                y_copies[k, d, s] = send(
                    block, block, y_send.at[slot], y_recv.at[slot], tensor_peer(s)
                )
                sent.append(y_copies[k, d, s])

    def share_on(m):
        for f in range(1, mid):
            g_copies[m, f, 0].wait_recv()
            for e in range(1, inner):
                share(m, f, e, (0, e))

    def own_part(m):
        for f in range(mid):
            for e in range(1, inner):
                g_copies[m, f, e].wait_recv()
        total = None
        for g in range(group):
            term = jnp.dot(
                xin[a, :, g * rows:(g + 1) * rows], mg[g, m], preferred_element_type=F32
            )
            total = term if total is None else total + term
        acc[m] = total

    p_copies = {}

    def give(k, m, d, to):
        slot = (d * pieces + k) * mats + m
        p_copies[k, m, d] = send(
            pout.at[d, m, some(k)], pin.at[d, m, some(k)],
            p_send.at[slot], p_recv.at[slot], at(flip(a, to), b, c),
        )
        sent.append(p_copies[k, m, d])

    def parts(k, m):
        if m == 0:
            for d in turns:
                for s in range(1, n_tensor):
                    y_copies[k, d, s].wait_recv()
        if not turns:
            return
        total = None
        for g in range(group):
            left = jnp.concatenate(
                [xin[flip(a, d), some(k), g * rows:(g + 1) * rows] for d in turns], axis=0
            )
            term = jnp.dot(left, mg[g, m], preferred_element_type=F32)
            total = term if total is None else total + term
        for n, d in enumerate(turns):
            mine_part = total[n * piece:(n + 1) * piece]
            if d == 2:
                hold[m, some(k)] = mine_part
            else:
                pout[d, m, some(k)] = mine_part.astype(BF16)
                give(k, m, d, 1)

    def combine(k, m):
        if 2 not in turns:
            return
        p_copies[k, m, 3].wait_recv()
        pout[2, m, some(k)] = (hold[m, some(k)] + pin[3, m, some(k)].astype(F32)).astype(BF16)
        give(k, m, 2, 2)

    last = pieces - 1
    pass_on(0)
    own_copy.wait()
    for k in range(pieces):
        spread(k, 0)
    share_on(0)
    for k in range(1, last):
        pass_on(k)
    own_part(0)
    for k in range(last):
        parts(k, 0)
        if k:
            combine(k - 1, 0)
    share_on(1)
    if last:
        pass_on(last)
        combine(last - 1, 0)
    parts(last, 0)
    own_part(1)
    parts(0, 1)
    combine(last, 0)
    for k in range(1, pieces):
        parts(k, 1)
        combine(k - 1, 1)
        for d in turns:
            spread(k - 1, d)
    combine(last, 1)
    for d in turns:
        spread(last, d)
    for m in range(mats):
        for k in range(pieces):
            total = acc[m, some(k)]
            for d in turns:
                if d < 3:
                    p_copies[k, m, d].wait_recv()
                    total = total + pin[d, m, some(k)].astype(F32)
            kv_out[m, some(k)] = total.astype(BF16)
    for copy in keeps:
        copy.wait()
    for copy in r_copies:
        copy.wait_recv()
    for copy in sent + r_copies:
        copy.wait_send()


def project(dims, n_tensor, inputs, vectors, base, exps, coefs):
    outer, mid, inner = dims
    group = mid * inner
    tokens = inputs.shape[0]
    _, mats, rows, cols = vectors.shape
    span = group * rows
    pieces = math.gcd(tokens // 16, 3)
    dma = pltpu.SemaphoreType.DMA
    count = outer * group
    hbm = pl.BlockSpec(memory_space=pl.ANY)
    smem = pl.BlockSpec(memory_space=pltpu.SMEM)
    return pl.pallas_call(
        functools.partial(project_kernel, dims, n_tensor, pieces),
        out_shape=(
            jax.ShapeDtypeStruct((mats, tokens, cols), BF16),
            jax.ShapeDtypeStruct((count, tokens, rows), BF16),
        ),
        in_specs=[hbm, hbm, hbm, smem, smem],
        out_specs=(pl.BlockSpec(memory_space=pltpu.VMEM), hbm),
        scratch_shapes=[
            pltpu.VMEM((outer, tokens, span), BF16),
            pltpu.VMEM((group, mats, rows, cols), BF16),
            pltpu.VMEM(vectors.shape, BF16),
            pltpu.VMEM(base.shape, BF16),
            pltpu.VMEM((mats, tokens, cols), F32),
            pltpu.VMEM((mats, tokens, cols), F32),
            pltpu.VMEM((outer, mats, tokens, cols), BF16),
            pltpu.VMEM((outer, mats, tokens, cols), BF16),
            dma((2 + mats,)), dma((pieces * outer,)),
            dma((outer * pieces,)), dma((outer * pieces,)),
            dma((pieces * outer * n_tensor,)), dma((pieces * outer * n_tensor,)),
            dma((mats * group,)), dma((mats * group,)),
            dma((pieces * count,)), dma((pieces * count,)),
            dma((outer * pieces * mats,)), dma((outer * pieces * mats,)),
        ],
        compiler_params=pltpu.CompilerParams(
            collective_id=0, has_side_effects=True, vmem_limit_bytes=VMEM_BYTES
        ),
        name="project",
    )(inputs, vectors, base, exps, coefs)


def attend_kernel(
    n_tensor, queries, kv, att_out, dkv_out, ent_out, probs, logs, expos, sums, s_send, s_recv
):
    task = lax.axis_index("task")
    y = lax.axis_index("tensor")
    tokens = queries.shape[0]
    heads = kv.shape[2] // HEAD
    inverse = HEAD ** (-0.5)
    peers = [{"task": task, "tensor": turned(y, s, n_tensor)} for s in range(1, n_tensor)]
    if peers:
        meet(peers)
    key_at = lax.broadcasted_iota(jnp.int32, (tokens, GROUP * tokens), 0)
    query_at = lax.rem(lax.broadcasted_iota(jnp.int32, (tokens, GROUP * tokens), 1), tokens)
    causal = key_at <= query_at

    def stacked(h):
        return jnp.concatenate(
            [queries[:, (h * GROUP + r) * HEAD:(h * GROUP + r + 1) * HEAD] for r in range(GROUP)],
            axis=0,
        )

    total = jnp.zeros((tokens, HEAD), F32)
    moment = jnp.zeros((tokens, HEAD), F32)
    for h in range(heads):
        cut = slice(h * HEAD, (h + 1) * HEAD)
        scores = lax.dot_general(
            kv[0, :, cut], stacked(h), (((1,), (1,)), ((), ())), preferred_element_type=F32
        ) * inverse
        scores = jnp.where(causal, scores, masked_value)
        weight = jnp.exp(scores - jnp.max(scores, axis=0, keepdims=True))
        prob = weight * (1.0 / jnp.sum(weight, axis=0, keepdims=True))
        probs[h] = prob
        att = lax.dot_general(
            prob.astype(BF16), kv[1, :, cut], (((0,), (0,)), ((), ())), preferred_element_type=F32
        ).astype(BF16)
        logits = capping * jnp.tanh(sharpen * att.astype(F32) / capping)
        expo = jnp.exp(logits)
        logs[h] = logits
        expos[h] = expo
        scaled = expo * logits
        for r in range(GROUP):
            here = slice(r * tokens, (r + 1) * tokens)
            att_out[:, (h * GROUP + r) * HEAD:(h * GROUP + r + 1) * HEAD] = att[here]
            total += expo[here]
            moment += scaled[here]
    sums[y] = jnp.concatenate(
        [
            jnp.sum(total.T, axis=0, keepdims=True),
            jnp.sum(moment.T, axis=0, keepdims=True),
            jnp.zeros((6, tokens), F32),
        ],
        axis=0,
    )
    copies = [
        send(sums.at[y], sums.at[y], s_send.at[s], s_recv.at[s], peer)
        for s, peer in enumerate(peers)
    ]
    for copy in copies:
        copy.wait_recv()
    whole = sums[0]
    for s in range(1, n_tensor):
        whole = whole + sums[s]
    over = 1.0 / whole[0:1]
    average = whole[1:2] * over
    ent_out[...] = jnp.log(whole[0:1]) - average
    over_col = jnp.broadcast_to(over, (HEAD, tokens)).T
    average_col = jnp.broadcast_to(average, (HEAD, tokens)).T
    over_all = jnp.concatenate([over_col] * GROUP, axis=0)
    average_all = jnp.concatenate([average_col] * GROUP, axis=0)
    for h in range(heads):
        cut = slice(h * HEAD, (h + 1) * HEAD)
        logits = logs[h]
        slope = sharpen * (1.0 - (logits / capping) ** 2)
        d_out = (slope * (-(expos[h] * over_all) * (logits - average_all))).astype(BF16)
        prob = probs[h]
        d_probs = lax.dot_general(
            kv[1, :, cut], d_out, (((1,), (1,)), ((), ())), preferred_element_type=F32
        )
        d_scores = (
            prob * (d_probs - jnp.sum(prob * d_probs, axis=0, keepdims=True))
        ).astype(BF16)
        d_keys = jnp.dot(d_scores, stacked(h), preferred_element_type=F32) * inverse
        d_values = jnp.dot(prob.astype(BF16), d_out, preferred_element_type=F32)
        dkv_out[0, :, cut] = d_keys.astype(BF16)
        dkv_out[1, :, cut] = d_values.astype(BF16)
    for copy in copies:
        copy.wait_send()


def attend(n_tensor, queries, kv):
    tokens = queries.shape[0]
    heads = kv.shape[2] // HEAD
    vmem = pl.BlockSpec(memory_space=pltpu.VMEM)
    dma = pltpu.SemaphoreType.DMA
    return pl.pallas_call(
        functools.partial(attend_kernel, n_tensor),
        out_shape=(
            jax.ShapeDtypeStruct(queries.shape, BF16),
            jax.ShapeDtypeStruct(kv.shape, BF16),
            jax.ShapeDtypeStruct((1, tokens), F32),
        ),
        in_specs=[vmem, vmem],
        out_specs=(vmem, vmem, vmem),
        scratch_shapes=[
            pltpu.VMEM((heads, tokens, GROUP * tokens), F32),
            pltpu.VMEM((heads, GROUP * tokens, HEAD), F32),
            pltpu.VMEM((heads, GROUP * tokens, HEAD), F32),
            pltpu.VMEM((n_tensor, 8, tokens), F32),
            dma((n_tensor,)), dma((n_tensor,)),
        ],
        compiler_params=pltpu.CompilerParams(
            collective_id=1, has_side_effects=True, vmem_limit_bytes=VMEM_BYTES
        ),
        name="attend",
    )(queries, kv)


def reduce_kernel(
    dims, n_tensor,
    dkv, rows_in, vectors, exps, ent, out,
    got, rows_v, vec_v, grads, held, held_t,
    local_sem, g_send, g_recv, t_send, t_recv, y_send, y_recv,
):
    outer, mid, inner = dims
    n_task = outer * mid * inner
    task, a, b, c = place(dims)
    y = lax.axis_index("tensor")
    tasks, mats, rows, cols = vectors.shape
    row_blocks, col_blocks = exps.shape[2:]
    near = [d for d in (2, 3, 1) if d < outer]
    order = [0] + near

    rows_copy = fetch(rows_in, rows_v, local_sem.at[0])
    vec_copy = fetch(vectors, vec_v, local_sem.at[1])

    def to(d, f, e):
        spot = index_of(dims, flip(a, d), turned(b, f, mid), turned(c, e, inner))
        return {"task": spot, "tensor": y}

    def source(d, f, e):
        return index_of(dims, flip(a, d), turned(b, -f, mid), turned(c, -e, inner))

    task_peers = [{"task": turned(task, s, n_task), "tensor": y} for s in range(1, n_task)]
    tensor_peers = [{"task": task, "tensor": turned(y, s, n_tensor)} for s in range(1, n_tensor)]
    meet(task_peers + tensor_peers)
    copies = {}

    def forward(m, held_at, hop):
        where = source(*held_at)
        slot = tuple(p + q for p, q in zip(held_at, hop))
        flat = ((m * outer + slot[0]) * mid + slot[1]) * inner + slot[2]
        copies[m, slot] = send(
            got.at[m, where] if any(held_at) else dkv.at[m],
            got.at[m, where],
            g_send.at[flat], g_recv.at[flat], to(*hop),
        )

    def take(m, slot):
        if any(slot):
            copies[m, slot].wait_recv()
        d, f, e = slot
        if not e:
            if not f:
                for step in range(1, mid):
                    forward(m, slot, (0, step, 0))
            for step in range(1, inner):
                forward(m, slot, (0, 0, step))
        where = source(*slot)
        block = got[m, where] if any(slot) else dkv[m]
        term = lax.dot_general(
            rows_v[where], block, (((0,), (0,)), ((), ())), preferred_element_type=F32
        )
        if any(slot):
            grads[m] += term
        else:
            grads[m] = term

    for m in range(mats):
        for d in near:
            forward(m, (0, 0, 0), (d, 0, 0))
    high = rows // row_blocks
    wide = cols // col_blocks

    def contracted(m):
        def contract(i, carry):
            these = pl.ds(pl.multiple_of(i * high, 8), high)
            carry = list(carry)
            for j in range(col_blocks):
                across = slice(j * wide, (j + 1) * wide)
                grad = grads[m, these, across]
                for t in range(tasks):
                    term = grad * vec_v[t, m, these, across].astype(F32)
                    term = jnp.sum(term.reshape(high // 8, 8, wide), axis=0)
                    carry[t] = carry[t] + scale_of(exps, t, m, i, j) * term
            return tuple(carry)

        start = tuple(jnp.zeros((8, wide), F32) for _ in range(tasks))
        return lax.fori_loop(0, row_blocks, contract, start)

    rows_copy.wait()
    lines = []
    for step in range(mats * outer + 2):
        if step == outer + 2:
            vec_copy.wait()
        if step > outer and (step - 2) % outer == 0:
            lines.append(contracted((step - 2) // outer - 1))
        slots = []
        if step < mats * outer:
            slots.append((step, 0, 0))
        if 1 <= step <= mats * outer:
            slots += [(step - 1, f, 0) for f in range(1, mid)]
            slots += [(step - 1, 0, e) for e in range(1, inner)]
        if step >= 2:
            slots += [(step - 2, f, e) for f in range(1, mid) for e in range(1, inner)]
        for at_step, f, e in slots:
            take(at_step // outer, (order[at_step % outer], f, e))
    while len(lines) < mats:
        if not lines:
            vec_copy.wait()
        lines.append(contracted(len(lines)))
    parts = [
        jnp.sum(lines[m][t], axis=0, keepdims=True) for t in range(tasks) for m in range(mats)
    ]
    entropy = jnp.broadcast_to(jnp.sum(ent[...]) / (n_tensor * wide), (1, wide))
    pad = -(len(parts) + 1) % 8
    stack = jnp.concatenate(parts + [entropy, jnp.zeros((pad, wide), F32)], axis=0)
    column = jnp.sum(stack, axis=1, keepdims=True)
    shape = (stack.shape[0], held.shape[2])
    along = lax.broadcasted_iota(jnp.int32, shape, 0) == lax.broadcasted_iota(jnp.int32, shape, 1)
    line = jnp.sum(jnp.where(along, column, 0.0), axis=0, keepdims=True)
    held[task] = jnp.broadcast_to(line, held.shape[1:])
    last = [
        send(held.at[task], held.at[task], t_send.at[s], t_recv.at[s], peer)
        for s, peer in enumerate(task_peers)
    ]
    for copy in last:
        copy.wait_recv()
    total = held[0]
    for k in range(1, n_task):
        total = total + held[k]
    held_t[y] = total
    more = [
        send(held_t.at[y], held_t.at[y], y_send.at[s], y_recv.at[s], peer)
        for s, peer in enumerate(tensor_peers)
    ]
    for copy in more:
        copy.wait_recv()
    total = held_t[0]
    for k in range(1, n_tensor):
        total = total + held_t[k]
    out[...] = total
    for copy in list(copies.values()) + last + more:
        copy.wait_send()


def reduce(dims, n_tensor, dkv, rows_in, vectors, exps, ent):
    n_task, tokens, rows = rows_in.shape
    tasks, mats, _, cols = vectors.shape
    vmem = pl.BlockSpec(memory_space=pltpu.VMEM)
    hbm = pl.BlockSpec(memory_space=pl.ANY)
    dma = pltpu.SemaphoreType.DMA
    return pl.pallas_call(
        functools.partial(reduce_kernel, dims, n_tensor),
        out_shape=jax.ShapeDtypeStruct((8, 128), F32),
        in_specs=[vmem, hbm, hbm, pl.BlockSpec(memory_space=pltpu.SMEM), vmem],
        out_specs=vmem,
        scratch_shapes=[
            pltpu.VMEM((mats, n_task, tokens, cols), BF16),
            pltpu.VMEM((n_task, tokens, rows), BF16),
            pltpu.VMEM(vectors.shape, BF16),
            pltpu.VMEM((mats, rows, cols), F32),
            pltpu.VMEM((n_task, 8, 128), F32),
            pltpu.VMEM((n_tensor, 8, 128), F32),
            dma((2,)),
            dma((mats * n_task,)), dma((mats * n_task,)),
            dma((n_task,)), dma((n_task,)),
            dma((n_tensor,)), dma((n_tensor,)),
        ],
        compiler_params=pltpu.CompilerParams(
            collective_id=2, has_side_effects=True, vmem_limit_bytes=VMEM_BYTES
        ),
        name="reduce",
    )(dkv, rows_in, vectors, exps, ent)


def local(inputs, queries, task_vectors, base_weights, scale_exps, coefs):
    n_task = lax.axis_size("task")
    n_tensor = lax.axis_size("tensor")
    dims = factors(n_task)
    tasks, mats = coefs.shape
    kv, rows_in = project(
        dims, n_tensor, inputs, task_vectors, base_weights, scale_exps, coefs
    )
    attended, dkv, ent = attend(n_tensor, queries, kv)
    sums = reduce(dims, n_tensor, dkv, rows_in, task_vectors, scale_exps, ent)
    coef_grad = sums[0, : tasks * mats].reshape(tasks, mats)
    mean_entropy = sums[0, tasks * mats] / (inputs.shape[0] * n_task)
    return (attended, mean_entropy, coef_grad)


def solution(mesh):
    return jax.shard_map(
        local,
        mesh=mesh,
        in_specs=(
            P("task", None),
            P("task", "tensor"),
            P(None, None, "task", "tensor"),
            P(None, "task", "tensor"),
            P(None, None, "task", "tensor"),
            P(),
        ),
        out_specs=(P("task", "tensor"), P(), P()),
        check_vma=False,
    )
```

time: 173 us -> 173 us (level)
    unnamed x4 -> x6, local copies, waits for them, and re-layouts: 1.53 us -> 4.31 us
where the time goes in v2:
time: 173 us; the launch traced here: 172 us
  Pallas kernels  164 us (95%)
  local copies, waits for them, and re-layouts  6.34 us (4%)
  between operations  2.45 us (1%)
    pallas_call x1, Pallas kernels, project(): pl.pallas_call(functools.partial(project_kernel, dims, n_tensor, pieces),...  84.4 us
    pallas_call x1, Pallas kernels, reduce(): pl.pallas_call(functools.partial(reduce_kernel, dims, n_tensor), out_shap...  69.5 us
    pallas_call x1, Pallas kernels, attend(): pl.pallas_call(functools.partial(attend_kernel, n_tensor), out_shape=(jax...  9.75 us
    unnamed x6, local copies, waits for them, and re-layouts  4.31 us

profile of v2, /device:TPU:0, one launch (start us, length us, event | category | flops | bytes accessed | tf_op | source)
XLA Modules:
  0.0 172.5 jit_solution(1381006449646165012)
XLA Ops:
  0.6 1.3 copy.14.coefs
  2.0 1.4 copy.13.exps
  3.4 84.4 %project.1 = (bf16[2,192,512]{2,1,0:T(8,128)(2,1)}, bf16[16,192,512]{2,1,0:T(8,128)(2,1)}) custom-call(bf16[192,8192]{1,0:T(8,128)(2,1)} %inputs.1, bf16[8,2,512,512]{3,2,1,0:T(8,128)(2,1)} %vectors.3, bf16[2,512,512]{2,1,0:T(8,128)(2,1)} %base.1, s32[8,2,4,4]{3,2,1,0:T(4,128)} %copy.13.exps, f32[8,2]{1,0:T(8,128)} %copy.14.coefs), custom_call_target="tpu_custom_call" | custom-call | tf_op jit(solution)/shard_map/project/pallas_call | solution.py:328
  87.9 9.7 %attend.1 = (bf16[192,2048]{1,0:T(8,128)(2,1)}, bf16[2,192,512]{2,1,0:T(8,128)(2,1)}, f32[1,192]{1,0:T(1,128)}) custom-call(bf16[192,2048]{1,0:T(8,128)(2,1)} %queries.1, bf16[2,192,512]{2,1,0:T(8,128)(2,1)} %get-tuple-element.8.kv), custom_call_target="tpu_custom_call" | custom-call | tf_op jit(solution)/shard_map/attend/pallas_call | solution.py:453
  97.6 0.0 copy-start
  97.6 69.5 %reduce.5 = f32[8,128]{1,0:T(8,128)} custom-call(bf16[2,192,512]{2,1,0:T(8,128)(2,1)} %get-tuple-element.10.dkv, bf16[16,192,512]{2,1,0:T(8,128)(2,1)} %get-tuple-element.11.rows_in, bf16[8,2,512,512]{3,2,1,0:T(8,128)(2,1)} %vectors.3, s32[8,2,4,4]{3,2,1,0:T(4,128)} %copy.13.exps, f32[1,192]{1,0:T(1,128)} %get-tuple-element.12.ent), custom_call_target="tpu_custom_call" | custom-call | tf_op jit(solution)/shard_map/reduce/pallas_call | solution.py:620
  167.1 1.3 slice.6
  169.0 0.7 slice_reduce_fusion
  169.7 0.1 reshape_squeeze.3
  169.8 0.6 copy.16
  170.5 0.0 copy-done
  170.5 0.9 copy.18
Async XLA Ops:
  97.6 72.8 %copy-start = (bf16[192,2048]{1,0:T(8,128)(2,1)S(1)}, bf16[192,2048]{1,0:T(8,128)(2,1)}, u32[]{:S(2)}) copy-start(bf16[192,2048]{1,0:T(8,128)(2,1)} %get-tuple-element.22) | copy-start | bytes 2359300

commit v3 on v2

--- a/solution.py
+++ b/solution.py
@@ -83,9 +83,9 @@
     return copy
 
 
-def project_kernel(
+def project_stage(
     dims, n_tensor, pieces,
-    inputs, vectors, base, exps, coefs,
+    inputs, vectors, base, exps, coefs, greet,
     kv_out, rows_out,
     xin, mg, vec_v, base_v, acc, hold, pout, pin,
     local_sem, keep_sem, x_send, x_recv, y_send, y_recv, g_send, g_recv, r_send, r_recv, p_send, p_recv,
@@ -115,9 +115,6 @@
     def some(k):
         return slice(k * piece, (k + 1) * piece)
 
-    peers = [at(flip(a, d), b, c) for d in turns]
-    peers += [group_peer(f, e) for f in range(mid) for e in range(inner) if f or e]
-    peers += [tensor_peer(s) for s in range(1, n_tensor)]
     base_copy = fetch(base, base_v, local_sem.at[0])
     vec_copies = [
         fetch(vectors.at[:, m], vec_v.at[:, m], local_sem.at[2 + m]) for m in range(mats)
@@ -125,7 +122,7 @@
     own_copy = fetch(
         inputs.at[:, pl.ds(pl.multiple_of(a * span, 128), span)], xin.at[a], local_sem.at[1]
     )
-    meet(peers)
+    greet()
     sent = []
     x_copies = {}
     own_cols = pl.ds(pl.multiple_of(y * part, 128), part)
@@ -282,6 +279,8 @@
         parts(k, 0)
         if k:
             combine(k - 1, 0)
+        for d in turns:
+            spread(k, d)
     share_on(1)
     if last:
         pass_on(last)
@@ -293,8 +292,6 @@
     for k in range(1, pieces):
         parts(k, 1)
         combine(k - 1, 1)
-        for d in turns:
-            spread(k - 1, d)
     combine(last, 1)
     for d in turns:
         spread(last, d)
@@ -306,58 +303,11 @@
                     p_copies[k, m, d].wait_recv()
                     total = total + pin[d, m, some(k)].astype(F32)
             kv_out[m, some(k)] = total.astype(BF16)
-    for copy in keeps:
-        copy.wait()
-    for copy in r_copies:
-        copy.wait_recv()
-    for copy in sent + r_copies:
-        copy.wait_send()
-
-
-def project(dims, n_tensor, inputs, vectors, base, exps, coefs):
-    outer, mid, inner = dims
-    group = mid * inner
-    tokens = inputs.shape[0]
-    _, mats, rows, cols = vectors.shape
-    span = group * rows
-    pieces = math.gcd(tokens // 16, 3)
-    dma = pltpu.SemaphoreType.DMA
-    count = outer * group
-    hbm = pl.BlockSpec(memory_space=pl.ANY)
-    smem = pl.BlockSpec(memory_space=pltpu.SMEM)
-    return pl.pallas_call(
-        functools.partial(project_kernel, dims, n_tensor, pieces),
-        out_shape=(
-            jax.ShapeDtypeStruct((mats, tokens, cols), BF16),
-            jax.ShapeDtypeStruct((count, tokens, rows), BF16),
-        ),
-        in_specs=[hbm, hbm, hbm, smem, smem],
-        out_specs=(pl.BlockSpec(memory_space=pltpu.VMEM), hbm),
-        scratch_shapes=[
-            pltpu.VMEM((outer, tokens, span), BF16),
-            pltpu.VMEM((group, mats, rows, cols), BF16),
-            pltpu.VMEM(vectors.shape, BF16),
-            pltpu.VMEM(base.shape, BF16),
-            pltpu.VMEM((mats, tokens, cols), F32),
-            pltpu.VMEM((mats, tokens, cols), F32),
-            pltpu.VMEM((outer, mats, tokens, cols), BF16),
-            pltpu.VMEM((outer, mats, tokens, cols), BF16),
-            dma((2 + mats,)), dma((pieces * outer,)),
-            dma((outer * pieces,)), dma((outer * pieces,)),
-            dma((pieces * outer * n_tensor,)), dma((pieces * outer * n_tensor,)),
-            dma((mats * group,)), dma((mats * group,)),
-            dma((pieces * count,)), dma((pieces * count,)),
-            dma((outer * pieces * mats,)), dma((outer * pieces * mats,)),
-        ],
-        compiler_params=pltpu.CompilerParams(
-            collective_id=0, has_side_effects=True, vmem_limit_bytes=VMEM_BYTES
-        ),
-        name="project",
-    )(inputs, vectors, base, exps, coefs)
-
-
-def attend_kernel(
-    n_tensor, queries, kv, att_out, dkv_out, ent_out, probs, logs, expos, sums, s_send, s_recv
+    return sent + r_copies, r_copies, keeps
+
+
+def attend_stage(
+    n_tensor, queries, kv, att_out, dkv_out, probs, logs, expos, sums, s_send, s_recv
 ):
     task = lax.axis_index("task")
     y = lax.axis_index("tensor")
@@ -365,8 +315,6 @@
     heads = kv.shape[2] // HEAD
     inverse = HEAD ** (-0.5)
     peers = [{"task": task, "tensor": turned(y, s, n_tensor)} for s in range(1, n_tensor)]
-    if peers:
-        meet(peers)
     key_at = lax.broadcasted_iota(jnp.int32, (tokens, GROUP * tokens), 0)
     query_at = lax.rem(lax.broadcasted_iota(jnp.int32, (tokens, GROUP * tokens), 1), tokens)
     causal = key_at <= query_at
@@ -420,7 +368,7 @@
         whole = whole + sums[s]
     over = 1.0 / whole[0:1]
     average = whole[1:2] * over
-    ent_out[...] = jnp.log(whole[0:1]) - average
+    entropy = jnp.sum(jnp.log(whole[0:1]) - average)
     over_col = jnp.broadcast_to(over, (HEAD, tokens)).T
     average_col = jnp.broadcast_to(average, (HEAD, tokens)).T
     over_all = jnp.concatenate([over_col] * GROUP, axis=0)
@@ -441,55 +389,23 @@
         d_values = jnp.dot(prob.astype(BF16), d_out, preferred_element_type=F32)
         dkv_out[0, :, cut] = d_keys.astype(BF16)
         dkv_out[1, :, cut] = d_values.astype(BF16)
-    for copy in copies:
-        copy.wait_send()
-
-
-def attend(n_tensor, queries, kv):
-    tokens = queries.shape[0]
-    heads = kv.shape[2] // HEAD
-    vmem = pl.BlockSpec(memory_space=pltpu.VMEM)
-    dma = pltpu.SemaphoreType.DMA
-    return pl.pallas_call(
-        functools.partial(attend_kernel, n_tensor),
-        out_shape=(
-            jax.ShapeDtypeStruct(queries.shape, BF16),
-            jax.ShapeDtypeStruct(kv.shape, BF16),
-            jax.ShapeDtypeStruct((1, tokens), F32),
-        ),
-        in_specs=[vmem, vmem],
-        out_specs=(vmem, vmem, vmem),
-        scratch_shapes=[
-            pltpu.VMEM((heads, tokens, GROUP * tokens), F32),
-            pltpu.VMEM((heads, GROUP * tokens, HEAD), F32),
-            pltpu.VMEM((heads, GROUP * tokens, HEAD), F32),
-            pltpu.VMEM((n_tensor, 8, tokens), F32),
-            dma((n_tensor,)), dma((n_tensor,)),
-        ],
-        compiler_params=pltpu.CompilerParams(
-            collective_id=1, has_side_effects=True, vmem_limit_bytes=VMEM_BYTES
-        ),
-        name="attend",
-    )(queries, kv)
-
-
-def reduce_kernel(
-    dims, n_tensor,
-    dkv, rows_in, vectors, exps, ent, out,
+    return copies, entropy
+
+
+def reduce_stage(
+    dims, n_tensor, task_peers, tensor_peers, rows_ready, entropy,
+    dkv, exps, grad_out, mean_out,
     got, rows_v, vec_v, grads, held, held_t,
-    local_sem, g_send, g_recv, t_send, t_recv, y_send, y_recv,
+    g_send, g_recv, t_send, t_recv, y_send, y_recv,
 ):
     outer, mid, inner = dims
     n_task = outer * mid * inner
     task, a, b, c = place(dims)
     y = lax.axis_index("tensor")
-    tasks, mats, rows, cols = vectors.shape
+    tasks, mats, rows, cols = vec_v.shape
     row_blocks, col_blocks = exps.shape[2:]
-    near = [d for d in (2, 3, 1) if d < outer]
+    near = [d for d in (2, 1, 3) if d < outer]
     order = [0] + near
-
-    rows_copy = fetch(rows_in, rows_v, local_sem.at[0])
-    vec_copy = fetch(vectors, vec_v, local_sem.at[1])
 
     def to(d, f, e):
         spot = index_of(dims, flip(a, d), turned(b, f, mid), turned(c, e, inner))
@@ -498,9 +414,6 @@
     def source(d, f, e):
         return index_of(dims, flip(a, d), turned(b, -f, mid), turned(c, -e, inner))
 
-    task_peers = [{"task": turned(task, s, n_task), "tensor": y} for s in range(1, n_task)]
-    tensor_peers = [{"task": task, "tensor": turned(y, s, n_tensor)} for s in range(1, n_tensor)]
-    meet(task_peers + tensor_peers)
     copies = {}
 
     def forward(m, held_at, hop):
@@ -518,7 +431,7 @@
             copies[m, slot].wait_recv()
         d, f, e = slot
         if not e:
-            if not f:
+            if d and not f:
                 for step in range(1, mid):
                     forward(m, slot, (0, step, 0))
             for step in range(1, inner):
@@ -536,6 +449,8 @@
     for m in range(mats):
         for d in near:
             forward(m, (0, 0, 0), (d, 0, 0))
+        for step in range(1, mid):
+            forward(m, (0, 0, 0), (0, step, 0))
     high = rows // row_blocks
     wide = cols // col_blocks
 
@@ -555,11 +470,9 @@
         start = tuple(jnp.zeros((8, wide), F32) for _ in range(tasks))
         return lax.fori_loop(0, row_blocks, contract, start)
 
-    rows_copy.wait()
+    rows_ready()
     lines = []
     for step in range(mats * outer + 2):
-        if step == outer + 2:
-            vec_copy.wait()
         if step > outer and (step - 2) % outer == 0:
             lines.append(contracted((step - 2) // outer - 1))
         slots = []
@@ -573,13 +486,11 @@
         for at_step, f, e in slots:
             take(at_step // outer, (order[at_step % outer], f, e))
     while len(lines) < mats:
-        if not lines:
-            vec_copy.wait()
         lines.append(contracted(len(lines)))
     parts = [
         jnp.sum(lines[m][t], axis=0, keepdims=True) for t in range(tasks) for m in range(mats)
     ]
-    entropy = jnp.broadcast_to(jnp.sum(ent[...]) / (n_tensor * wide), (1, wide))
+    entropy = jnp.broadcast_to(entropy / (n_tensor * wide), (1, wide))
     pad = -(len(parts) + 1) % 8
     stack = jnp.concatenate(parts + [entropy, jnp.zeros((pad, wide), F32)], axis=0)
     column = jnp.sum(stack, axis=1, keepdims=True)
@@ -606,54 +517,131 @@
     total = held_t[0]
     for k in range(1, n_tensor):
         total = total + held_t[k]
-    out[...] = total
-    for copy in list(copies.values()) + last + more:
+    tokens = rows_v.shape[1]
+    mean_out[...] = total[0:1, tasks * mats:tasks * mats + 1] * (1.0 / (tokens * n_task))
+    line = jnp.broadcast_to(total[0:1], (tasks, total.shape[1]))
+    which = lax.broadcasted_iota(jnp.int32, line.shape, 1) - mats * lax.broadcasted_iota(
+        jnp.int32, line.shape, 0
+    )
+    at_mat = lax.broadcasted_iota(jnp.int32, (tasks, mats), 1)
+    result = jnp.zeros((tasks, mats), F32)
+    for m in range(mats):
+        column = jnp.sum(jnp.where(which == m, line, 0.0), axis=1, keepdims=True)
+        result = jnp.where(at_mat == m, column, result)
+    grad_out[...] = result
+    return list(copies.values()) + last + more
+
+
+def whole_kernel(
+    dims, n_tensor, pieces,
+    inputs, queries, vectors, base, exps, coefs,
+    att_hbm, mean_out, grad_out,
+    xin, mg, vec_v, base_v, acc, hold, pout, pin, kv, rows_v, att, dkv, probs, logs, expos, sums,
+    got, grads, held, held_t, out_sem,
+    local_sem, keep_sem, x_send, x_recv, y_send, y_recv, g_send, g_recv, r_send, r_recv, p_send, p_recv,
+    s_send, s_recv, d_send, d_recv, t_send, t_recv, z_send, z_recv,
+):
+    n_task = dims[0] * dims[1] * dims[2]
+    task = lax.axis_index("task")
+    y = lax.axis_index("tensor")
+    task_peers = [{"task": turned(task, s, n_task), "tensor": y} for s in range(1, n_task)]
+    tensor_peers = [{"task": task, "tensor": turned(y, s, n_tensor)} for s in range(1, n_tensor)]
+
+    def greet():
+        meet(task_peers + tensor_peers)
+
+    sent, r_copies, keeps = project_stage(
+        dims, n_tensor, pieces, inputs, vectors, base, exps, coefs, greet, kv, rows_v,
+        xin, mg, vec_v, base_v, acc, hold, pout, pin,
+        local_sem, keep_sem, x_send, x_recv, y_send, y_recv, g_send, g_recv, r_send, r_recv, p_send, p_recv,
+    )
+    exchanged, entropy = attend_stage(
+        n_tensor, queries, kv, att, dkv, probs, logs, expos, sums, s_send, s_recv
+    )
+    att_copy = fetch(att, att_hbm, out_sem)
+
+    def rows_ready():
+        for copy in keeps:
+            copy.wait()
+        for copy in r_copies:
+            copy.wait_recv()
+
+    more = reduce_stage(
+        dims, n_tensor, task_peers, tensor_peers, rows_ready, entropy, dkv, exps, grad_out, mean_out,
+        got, rows_v, vec_v, grads, held, held_t,
+        d_send, d_recv, t_send, t_recv, z_send, z_recv,
+    )
+    att_copy.wait()
+    for copy in sent + exchanged + more:
         copy.wait_send()
-
-
-def reduce(dims, n_tensor, dkv, rows_in, vectors, exps, ent):
-    n_task, tokens, rows = rows_in.shape
-    tasks, mats, _, cols = vectors.shape
-    vmem = pl.BlockSpec(memory_space=pltpu.VMEM)
-    hbm = pl.BlockSpec(memory_space=pl.ANY)
-    dma = pltpu.SemaphoreType.DMA
-    return pl.pallas_call(
-        functools.partial(reduce_kernel, dims, n_tensor),
-        out_shape=jax.ShapeDtypeStruct((8, 128), F32),
-        in_specs=[vmem, hbm, hbm, pl.BlockSpec(memory_space=pltpu.SMEM), vmem],
-        out_specs=vmem,
-        scratch_shapes=[
-            pltpu.VMEM((mats, n_task, tokens, cols), BF16),
-            pltpu.VMEM((n_task, tokens, rows), BF16),
-            pltpu.VMEM(vectors.shape, BF16),
-            pltpu.VMEM((mats, rows, cols), F32),
-            pltpu.VMEM((n_task, 8, 128), F32),
-            pltpu.VMEM((n_tensor, 8, 128), F32),
-            dma((2,)),
-            dma((mats * n_task,)), dma((mats * n_task,)),
-            dma((n_task,)), dma((n_task,)),
-            dma((n_tensor,)), dma((n_tensor,)),
-        ],
-        compiler_params=pltpu.CompilerParams(
-            collective_id=2, has_side_effects=True, vmem_limit_bytes=VMEM_BYTES
-        ),
-        name="reduce",
-    )(dkv, rows_in, vectors, exps, ent)
 
 
 def local(inputs, queries, task_vectors, base_weights, scale_exps, coefs):
     n_task = lax.axis_size("task")
     n_tensor = lax.axis_size("tensor")
     dims = factors(n_task)
-    tasks, mats = coefs.shape
-    kv, rows_in = project(
-        dims, n_tensor, inputs, task_vectors, base_weights, scale_exps, coefs
-    )
-    attended, dkv, ent = attend(n_tensor, queries, kv)
-    sums = reduce(dims, n_tensor, dkv, rows_in, task_vectors, scale_exps, ent)
-    coef_grad = sums[0, : tasks * mats].reshape(tasks, mats)
-    mean_entropy = sums[0, tasks * mats] / (inputs.shape[0] * n_task)
-    return (attended, mean_entropy, coef_grad)
+    outer, mid, inner = dims
+    group = mid * inner
+    tokens = inputs.shape[0]
+    tasks, mats, rows, cols = task_vectors.shape
+    heads = cols // HEAD
+    pieces = math.gcd(tokens // 16, 3)
+    hbm = pl.BlockSpec(memory_space=pl.ANY)
+    vmem = pl.BlockSpec(memory_space=pltpu.VMEM)
+    smem = pl.BlockSpec(memory_space=pltpu.SMEM)
+    dma = pltpu.SemaphoreType.DMA
+
+    def pair(count):
+        return [dma((count,)), dma((count,))]
+
+    attended, mean_entropy, coef_grad = pl.pallas_call(
+        functools.partial(whole_kernel, dims, n_tensor, pieces),
+        out_shape=(
+            jax.ShapeDtypeStruct(queries.shape, BF16),
+            jax.ShapeDtypeStruct((1, 1), F32),
+            jax.ShapeDtypeStruct((tasks, mats), F32),
+        ),
+        in_specs=[hbm, vmem, hbm, hbm, smem, smem],
+        out_specs=(hbm, vmem, vmem),
+        scratch_shapes=[
+            pltpu.VMEM((outer, tokens, group * rows), BF16),
+            pltpu.VMEM((group, mats, rows, cols), BF16),
+            pltpu.VMEM(task_vectors.shape, BF16),
+            pltpu.VMEM(base_weights.shape, BF16),
+            pltpu.VMEM((mats, tokens, cols), F32),
+            pltpu.VMEM((mats, tokens, cols), F32),
+            pltpu.VMEM((outer, mats, tokens, cols), BF16),
+            pltpu.VMEM((outer, mats, tokens, cols), BF16),
+            pltpu.VMEM((mats, tokens, cols), BF16),
+            pltpu.VMEM((n_task, tokens, rows), BF16),
+            pltpu.VMEM(queries.shape, BF16),
+            pltpu.VMEM((mats, tokens, cols), BF16),
+            pltpu.VMEM((heads, tokens, GROUP * tokens), F32),
+            pltpu.VMEM((heads, GROUP * tokens, HEAD), F32),
+            pltpu.VMEM((heads, GROUP * tokens, HEAD), F32),
+            pltpu.VMEM((n_tensor, 8, tokens), F32),
+            pltpu.VMEM((mats, n_task, tokens, cols), BF16),
+            pltpu.VMEM((mats, rows, cols), F32),
+            pltpu.VMEM((n_task, 8, 128), F32),
+            pltpu.VMEM((n_tensor, 8, 128), F32),
+            dma,
+            dma((2 + mats,)), dma((pieces * outer,)),
+            *pair(outer * pieces),
+            *pair(pieces * outer * n_tensor),
+            *pair(mats * group),
+            *pair(pieces * n_task),
+            *pair(outer * pieces * mats),
+            *pair(n_tensor),
+            *pair(mats * n_task),
+            *pair(n_task),
+            *pair(n_tensor),
+        ],
+        compiler_params=pltpu.CompilerParams(
+            collective_id=0, has_side_effects=True, vmem_limit_bytes=VMEM_BYTES
+        ),
+        name="whole",
+    )(inputs, queries, task_vectors, base_weights, scale_exps, coefs)
+    return (attended, mean_entropy[0, 0], coef_grad)
 
 
 def solution(mesh):

time: 173 us -> 147 us (0.85)
  Pallas kernels: 164 us -> 138 us
    pallas_call x3 -> x1, Pallas kernels: 164 us -> 138 us  [local(): pl.pallas_call(functools.partial(whole_kernel, dims, n_tensor, pieces), o...]
    slice x2 -> x0, local copies, waits for them, and re-layouts: 1.95 us -> none  [the longest x1 1.26 us: local(): mean_entropy = sums[0, tasks * mats] / (inputs.shape[0] * n_task)]
    unnamed x6 -> x4, local copies, waits for them, and re-layouts: 4.31 us -> 6.18 us
where the time goes in v3:
time: 147 us; the launch traced here: 146 us
  Pallas kernels  138 us (94%)
  local copies, waits for them, and re-layouts  6.18 us (4%)
  between operations  2.39 us (2%)
    pallas_call x1, Pallas kernels, local(): pl.pallas_call(functools.partial(whole_kernel, dims, n_tensor, pieces), o...  138 us
    unnamed x4, local copies, waits for them, and re-layouts  6.18 us

profile of v3, /device:TPU:0, one launch (start us, length us, event | category | flops | bytes accessed | tf_op | source)
XLA Modules:
  0.0 146.4 jit_solution(3757621049722671018)
XLA Ops:
  0.6 1.3 copy.10.coefs
  2.0 1.4 copy.9.exps
  3.4 137.9 %whole.1 = (bf16[192,2048]{1,0:T(8,128)(2,1)}, f32[1,1]{1,0:T(1,128)}, f32[8,2]{1,0:T(8,128)}) custom-call(bf16[192,8192]{1,0:T(8,128)(2,1)} %inputs.1, bf16[192,2048]{1,0:T(8,128)(2,1)} %queries.1, bf16[8,2,512,512]{3,2,1,0:T(8,128)(2,1)} %vectors.1, bf16[2,512,512]{2,1,0:T(8,128)(2,1)} %base.1, s32[8,2,4,4]{3,2,1,0:T(4,128)} %copy.9.exps, f32[8,2]{1,0:T(8,128)} %copy.10.coefs), custom_call_target="tpu_custom_call" | custom-call | tf_op jit(solution)/shard_map/whole/pallas_call | solution.py:597
  141.3 1.3 copy.11
  142.6 2.1 %copy.14 = bf16[192,2048]{1,0:T(8,128)(2,1)} copy(bf16[192,2048]{1,0:T(8,128)(2,1)} %get-tuple-element.15) | data formatting | bytes 1572864

commit v4 on v3

--- a/solution.py
+++ b/solution.py
@@ -49,7 +49,7 @@
 
 
 def scale_of(exps, t, m, i, j):
-    return lax.shift_left(jnp.int32(1), exps[t, m, i, j] + 3).astype(F32) * 0.125
+    return lax.shift_left(jnp.int32(1), exps[m, i, j, t] + 3).astype(F32) * 0.125
 
 
 def index_of(dims, a, b, c):
@@ -96,7 +96,7 @@
     y = lax.axis_index("tensor")
     mine = b * inner + c
     tasks, mats, rows, cols = vectors.shape
-    row_blocks, col_blocks = exps.shape[2:]
+    row_blocks, col_blocks = exps.shape[1:3]
     tokens = inputs.shape[0]
     piece = tokens // pieces
     span = group * rows
@@ -158,7 +158,7 @@
                 across = slice(j * wide, (j + 1) * wide)
                 total = base_v[m, these, across].astype(F32)
                 for t in range(tasks):
-                    scale = coefs[t, m] * scale_of(exps, t, m, i, j)
+                    scale = coefs[m, t] * scale_of(exps, t, m, i, j)
                     total += scale * vec_v[t, m, these, across].astype(F32)
                 mg[mine, m, these, across] = total.astype(BF16)
             return carry
@@ -403,7 +403,7 @@
     task, a, b, c = place(dims)
     y = lax.axis_index("tensor")
     tasks, mats, rows, cols = vec_v.shape
-    row_blocks, col_blocks = exps.shape[2:]
+    row_blocks, col_blocks = exps.shape[1:3]
     near = [d for d in (2, 1, 3) if d < outer]
     order = [0] + near
 
@@ -519,25 +519,26 @@
         total = total + held_t[k]
     tokens = rows_v.shape[1]
     mean_out[...] = total[0:1, tasks * mats:tasks * mats + 1] * (1.0 / (tokens * n_task))
-    line = jnp.broadcast_to(total[0:1], (tasks, total.shape[1]))
-    which = lax.broadcasted_iota(jnp.int32, line.shape, 1) - mats * lax.broadcasted_iota(
-        jnp.int32, line.shape, 0
-    )
-    at_mat = lax.broadcasted_iota(jnp.int32, (tasks, mats), 1)
-    result = jnp.zeros((tasks, mats), F32)
+    wide_line = jnp.broadcast_to(total[0:1], (tasks, total.shape[1]))
+    spot = lax.broadcasted_iota(jnp.int32, wide_line.shape, 1)
+    task_at = lax.broadcasted_iota(jnp.int32, wide_line.shape, 0)
+    grid = (mats, total.shape[1])
+    mat_at = lax.broadcasted_iota(jnp.int32, grid, 0)
+    result = jnp.zeros(grid, F32)
     for m in range(mats):
-        column = jnp.sum(jnp.where(which == m, line, 0.0), axis=1, keepdims=True)
-        result = jnp.where(at_mat == m, column, result)
-    grad_out[...] = result
+        column = jnp.sum(jnp.where(spot == mats * task_at + m, wide_line, 0.0), axis=1, keepdims=True)
+        row = jnp.sum(jnp.where(spot == task_at, column, 0.0), axis=0, keepdims=True)
+        result = jnp.where(mat_at == m, row, result)
+    grad_out[...] = result[:, :tasks]
     return list(copies.values()) + last + more
 
 
 def whole_kernel(
     dims, n_tensor, pieces,
     inputs, queries, vectors, base, exps, coefs,
-    att_hbm, mean_out, grad_out,
-    xin, mg, vec_v, base_v, acc, hold, pout, pin, kv, rows_v, att, dkv, probs, logs, expos, sums,
-    got, grads, held, held_t, out_sem,
+    att, mean_out, grad_out,
+    xin, mg, vec_v, base_v, acc, hold, pout, pin, kv, rows_v, dkv, probs, logs, expos, sums,
+    got, grads, held, held_t, smem_sem, exps_v, coefs_v,
     local_sem, keep_sem, x_send, x_recv, y_send, y_recv, g_send, g_recv, r_send, r_recv, p_send, p_recv,
     s_send, s_recv, d_send, d_recv, t_send, t_recv, z_send, z_recv,
 ):
@@ -547,18 +548,21 @@
     task_peers = [{"task": turned(task, s, n_task), "tensor": y} for s in range(1, n_task)]
     tensor_peers = [{"task": task, "tensor": turned(y, s, n_tensor)} for s in range(1, n_tensor)]
 
+    small = [fetch(exps, exps_v, smem_sem.at[0]), fetch(coefs, coefs_v, smem_sem.at[1])]
+
     def greet():
         meet(task_peers + tensor_peers)
+        for copy in small:
+            copy.wait()
 
     sent, r_copies, keeps = project_stage(
-        dims, n_tensor, pieces, inputs, vectors, base, exps, coefs, greet, kv, rows_v,
+        dims, n_tensor, pieces, inputs, vectors, base, exps_v, coefs_v, greet, kv, rows_v,
         xin, mg, vec_v, base_v, acc, hold, pout, pin,
         local_sem, keep_sem, x_send, x_recv, y_send, y_recv, g_send, g_recv, r_send, r_recv, p_send, p_recv,
     )
     exchanged, entropy = attend_stage(
         n_tensor, queries, kv, att, dkv, probs, logs, expos, sums, s_send, s_recv
     )
-    att_copy = fetch(att, att_hbm, out_sem)
 
     def rows_ready():
         for copy in keeps:
@@ -567,11 +571,10 @@
             copy.wait_recv()
 
     more = reduce_stage(
-        dims, n_tensor, task_peers, tensor_peers, rows_ready, entropy, dkv, exps, grad_out, mean_out,
+        dims, n_tensor, task_peers, tensor_peers, rows_ready, entropy, dkv, exps_v, grad_out, mean_out,
         got, rows_v, vec_v, grads, held, held_t,
         d_send, d_recv, t_send, t_recv, z_send, z_recv,
     )
-    att_copy.wait()
     for copy in sent + exchanged + more:
         copy.wait_send()
 
@@ -588,7 +591,6 @@
     pieces = math.gcd(tokens // 16, 3)
     hbm = pl.BlockSpec(memory_space=pl.ANY)
     vmem = pl.BlockSpec(memory_space=pltpu.VMEM)
-    smem = pl.BlockSpec(memory_space=pltpu.SMEM)
     dma = pltpu.SemaphoreType.DMA
 
     def pair(count):
@@ -599,10 +601,10 @@
         out_shape=(
             jax.ShapeDtypeStruct(queries.shape, BF16),
             jax.ShapeDtypeStruct((1, 1), F32),
-            jax.ShapeDtypeStruct((tasks, mats), F32),
+            jax.ShapeDtypeStruct((mats, tasks), F32),
         ),
-        in_specs=[hbm, vmem, hbm, hbm, smem, smem],
-        out_specs=(hbm, vmem, vmem),
+        in_specs=[hbm, vmem, hbm, hbm, hbm, hbm],
+        out_specs=(vmem, vmem, vmem),
         scratch_shapes=[
             pltpu.VMEM((outer, tokens, group * rows), BF16),
             pltpu.VMEM((group, mats, rows, cols), BF16),
@@ -614,7 +616,6 @@
             pltpu.VMEM((outer, mats, tokens, cols), BF16),
             pltpu.VMEM((mats, tokens, cols), BF16),
             pltpu.VMEM((n_task, tokens, rows), BF16),
-            pltpu.VMEM(queries.shape, BF16),
             pltpu.VMEM((mats, tokens, cols), BF16),
             pltpu.VMEM((heads, tokens, GROUP * tokens), F32),
             pltpu.VMEM((heads, GROUP * tokens, HEAD), F32),
@@ -624,7 +625,8 @@
             pltpu.VMEM((mats, rows, cols), F32),
             pltpu.VMEM((n_task, 8, 128), F32),
             pltpu.VMEM((n_tensor, 8, 128), F32),
-            dma,
+            dma((2,)),
+            pltpu.SMEM((mats, *scale_exps.shape[2:], tasks), jnp.int32), pltpu.SMEM((mats, tasks), F32),
             dma((2 + mats,)), dma((pieces * outer,)),
             *pair(outer * pieces),
             *pair(pieces * outer * n_tensor),
@@ -640,8 +642,8 @@
             collective_id=0, has_side_effects=True, vmem_limit_bytes=VMEM_BYTES
         ),
         name="whole",
-    )(inputs, queries, task_vectors, base_weights, scale_exps, coefs)
-    return (attended, mean_entropy[0, 0], coef_grad)
+    )(inputs, queries, task_vectors, base_weights, scale_exps.transpose(1, 2, 3, 0), coefs.T)
+    return (attended, mean_entropy[0, 0], coef_grad.T)
 
 
 def solution(mesh):

time: 147 us -> 144 us (0.980)
  local copies, waits for them, and re-layouts: 6.18 us -> 3.32 us
    unnamed x4 -> x2, local copies, waits for them, and re-layouts: 6.18 us -> 3.32 us
where the time goes in v4:
time: 144 us; the launch traced here: 143 us
  Pallas kernels  138 us (96%)
  local copies, waits for them, and re-layouts  3.32 us (2%)
  between operations  2.41 us (2%)
    pallas_call x1, Pallas kernels, local(): pl.pallas_call(functools.partial(whole_kernel, dims, n_tensor, pieces), o...  138 us
    unnamed x2, local copies, waits for them, and re-layouts  3.32 us

profile of v4, /device:TPU:0, one launch (start us, length us, event | category | flops | bytes accessed | tf_op | source)
XLA Modules:
  0.0 143.5 jit_solution(436938053842634852)
XLA Ops:
  0.6 137.7 %whole.1 = (bf16[192,2048]{1,0:T(8,128)(2,1)}, f32[1,1]{1,0:T(1,128)}, f32[2,8]{1,0:T(2,128)}) custom-call(bf16[192,8192]{1,0:T(8,128)(2,1)} %inputs.1, bf16[192,2048]{1,0:T(8,128)(2,1)} %queries.1, bf16[8,2,512,512]{3,2,1,0:T(8,128)(2,1)} %vectors.1, bf16[2,512,512]{2,1,0:T(8,128)(2,1)} %base.1, s32[2,4,4,8]{3,2,1,0:T(4,128)} %bitcast.4, f32[2,8]{1,0:T(2,128)} %bitcast.6), custom_call_target="tpu_custom_call" | custom-call | tf_op jit(solution)/shard_map/whole/pallas_call | solution.py:599
  138.4 2.1 %copy.12 = bf16[192,2048]{1,0:T(8,128)(2,1)} copy(bf16[192,2048]{1,0:T(8,128)(2,1)} %get-tuple-element.12) | data formatting | bytes 1572864
  141.1 1.2 copy.14
